TPU v7x, 128 devices: a whole 4x4x4 slice. The times are simulated.
128 devices in a mesh: req: 64 (over z, y, x), kv: 2 (over core).
Axes of the slice: x: 4, y: 4, z: 4, core: 2. Of those that a mesh axis runs over, the one named last changes fastest.
Arguments:
- queries: bfloat16 [16384, 2048], P(('req', 'kv')), may hold values from -6 to 6
- keys: bfloat16 [16384, 1024], P(('req', 'kv')), may hold values from -6 to 6
- values: bfloat16 [16384, 1024], P(('req', 'kv')), may hold values from -6 to 6
- residual: bfloat16 [16384, 3584], P(('req', 'kv'))
- segment_ids: int32 [16384], P(('req', 'kv')), may hold values from 127 to 16383, as said below
- regroup: int32 [16384], P(('req', 'kv')), may hold values from 0 to 16383, as said below
- out_weight: bfloat16 [2048, 3584], P('kv')
- attn_gain: float32 [3584], replicated, may hold values from 0.1 to 1.9
- pre_gain: float32 [3584], replicated, may hold values from 0.1 to 1.9
- gate_weight: bfloat16 [3584, 7168], P(None, 'kv'), may hold values from -0.09375 to 0.09375
- up_weight: bfloat16 [3584, 7168], P(None, 'kv'), may hold values from -0.09375 to 0.09375
- down_weight: bfloat16 [7168, 3584], P('kv')
- post_gain: float32 [3584], replicated, may hold values from 0.1 to 1.9
Outputs:
- layer_out: bfloat16 [16384, 3584], P(('req', 'kv'))
- key_cache_rows: bfloat16 [4, 16384, 256], P(None, ('req', 'kv'))
- value_cache_rows: bfloat16 [4, 16384, 256], P(None, ('req', 'kv'))
Inputs may be any that keep to these rules, and one draw needn't show every extreme that they name: `segment_ids`: A request is a run of consecutive slots carrying one id, the index of its last slot; no request runs from one index of req's 256 slots into the next. `regroup`: A permutation of the slots. Each device (in req+kv order) sends exactly one of its 128 slots to each of the 128 devices: for every pair of devices, exactly one slot of the first has its output row among the 128 rows of the second.
All inputs are finite; a program needn't handle non-finite values.
Results may differ from a plain program's by a relative error of at most 0.0095.
Values may be sent and summed in bfloat16 or wider, within the bound.
A program may use at most 192 MiB of HBM per device.

v0:
```python
import jax
import jax.numpy as jnp
from jax import lax
from jax.sharding import PartitionSpec as P

QUERY_HEADS = 8
KEY_VALUE_HEADS = 4
HEAD_ENTRIES = 256
WINDOW_REACH = 512


cap_value = 50.0
norm_eps = 1e-06


def from_behind(block, axis, distance):
    devices = range(lax.axis_size(axis))
    route = [(i - distance, i) for i in devices if i - distance in devices]
    return lax.ppermute(block, axis, route)


def rms_scale(values_in, gain_row):
    mean_square = jnp.mean(values_in * values_in, axis=-1, keepdims=True)
    return values_in * lax.rsqrt(mean_square + norm_eps) * gain_row


def key_mask(own_ids, key_ids, key_pos):
    distance = jnp.arange(own_ids.shape[0], dtype=jnp.int32)[:, None] - key_pos[None, :]
    return (own_ids[:, None] == key_ids[None, :]) & (distance >= 0) & (distance < WINDOW_REACH)


def block_terms(query_head_rows, key_heads, value_heads, allowed):
    raw_scores = jnp.einsum(
        "tkgd,skd->kgts", query_head_rows, key_heads, preferred_element_type=jnp.float32
    )
    scores = cap_value * jnp.tanh(raw_scores * HEAD_ENTRIES ** (-0.5) / cap_value)
    weights = jnp.where(allowed, jnp.exp(scores), 0.0)
    totals = jnp.sum(weights, axis=-1)
    numerator = jnp.einsum(
        "kgts,skd->tkgd",
        weights.astype(jnp.bfloat16),
        value_heads,
        preferred_element_type=jnp.float32,
    )
    return (numerator, totals)


def send_rows(normed_part, normed_pos, stream_part, key_portion, value_portion):
    received = (
        lax.all_to_all(normed_part, ("req", "kv"), split_axis=0, concat_axis=0, tiled=True),
        lax.all_to_all(normed_pos, ("req", "kv"), split_axis=0, concat_axis=0, tiled=True),
        lax.all_to_all(stream_part, ("req", "kv"), split_axis=0, concat_axis=0, tiled=True),
        lax.all_to_all(key_portion, ("req", "kv"), split_axis=0, concat_axis=0, tiled=True),
        lax.all_to_all(value_portion, ("req", "kv"), split_axis=0, concat_axis=0, tiled=True),
    )
    return received


def per_device(
    queries,
    keys,
    values,
    residual,
    segment_ids,
    regroup,
    out_weight,
    attn_gain,
    pre_gain,
    gate_weight,
    up_weight,
    down_weight,
    post_gain,
):
    resident_rows = queries.shape[0]
    grouped_heads = QUERY_HEADS // KEY_VALUE_HEADS
    query_head_rows = queries.reshape(resident_rows, KEY_VALUE_HEADS, grouped_heads, HEAD_ENTRIES)
    own_ids = segment_ids + 1
    base_pos = jnp.arange(resident_rows, dtype=jnp.int32)
    key_collections = [(keys, values, own_ids, base_pos)]
    moved_keys, moved_values, moved_ids = from_behind((keys, values, own_ids), "kv", 1)
    key_collections.append((moved_keys, moved_values, moved_ids, base_pos - resident_rows))
    gathered_keys = jnp.concatenate(
        [key_collection[0] for key_collection in key_collections], axis=0
    ).reshape(-1, KEY_VALUE_HEADS, HEAD_ENTRIES)
    gathered_values = jnp.concatenate(
        [key_collection[1] for key_collection in key_collections], axis=0
    ).reshape(-1, KEY_VALUE_HEADS, HEAD_ENTRIES)
    all_ids = jnp.concatenate([key_collection[2] for key_collection in key_collections], axis=0)
    all_pos = jnp.concatenate([key_collection[3] for key_collection in key_collections], axis=0)
    numerator, totals = block_terms(
        query_head_rows, gathered_keys, gathered_values, key_mask(own_ids, all_ids, all_pos)
    )
    attended_output = (
        (numerator / jnp.transpose(totals, (2, 0, 1))[..., None])
        .astype(jnp.bfloat16)
        .reshape(resident_rows, QUERY_HEADS * HEAD_ENTRIES)
    )
    head_rows = lax.all_to_all(attended_output, "kv", split_axis=1, concat_axis=0, tiled=True)
    picked = head_rows
    projected = lax.psum_scatter(
        jnp.dot(picked, out_weight, preferred_element_type=jnp.float32).astype(jnp.bfloat16),
        "kv",
        scatter_dimension=0,
        tiled=True,
    ).astype(jnp.float32)
    stream = (residual.astype(jnp.float32) + rms_scale(projected, attn_gain)).astype(jnp.bfloat16)
    normed = rms_scale(stream.astype(jnp.float32), pre_gain).astype(jnp.bfloat16)
    row_order = jnp.argsort(regroup)
    destination_rows = regroup[row_order]
    sorted_normed = normed[row_order]
    sorted_stream = stream[row_order]
    sorted_keys = keys[row_order]
    sorted_values = values[row_order]
    received = send_rows(
        sorted_normed, destination_rows % resident_rows, sorted_stream, sorted_keys, sorted_values
    )
    placed = jnp.argsort(received[1])
    own_normed = received[0][placed]
    group_normed = lax.all_gather(own_normed, "kv", axis=0, tiled=True)
    own_stream = received[2][placed]
    resident_keys = received[3][placed]
    resident_values = received[4][placed]
    picked = group_normed
    gate_part = jnp.dot(picked, gate_weight, preferred_element_type=jnp.float32)
    up_part = jnp.dot(picked, up_weight, preferred_element_type=jnp.float32)
    active = (jax.nn.gelu(gate_part, approximate=True) * up_part).astype(jnp.bfloat16)
    ffw_sum = lax.psum_scatter(
        jnp.dot(active, down_weight, preferred_element_type=jnp.float32).astype(jnp.bfloat16),
        "kv",
        scatter_dimension=0,
        tiled=True,
    ).astype(jnp.float32)
    layer_out = (own_stream.astype(jnp.float32) + rms_scale(ffw_sum, post_gain)).astype(
        jnp.bfloat16
    )
    key_cache_rows = resident_keys.reshape(resident_rows, KEY_VALUE_HEADS, HEAD_ENTRIES).transpose(
        1, 0, 2
    )
    value_cache_rows = resident_values.reshape(
        resident_rows, KEY_VALUE_HEADS, HEAD_ENTRIES
    ).transpose(1, 0, 2)
    return (layer_out, key_cache_rows, value_cache_rows)


def solution(mesh):
    placed = (
        P(("req", "kv"), None),
        P(("req", "kv"), None),
        P(("req", "kv"), None),
        P(("req", "kv"), None),
        P(("req", "kv")),
        P(("req", "kv")),
        P("kv", None),
        P(),
        P(),
        P(None, "kv"),
        P(None, "kv"),
        P("kv", None),
        P(),
    )
    return jax.shard_map(
        per_device,
        mesh=mesh,
        in_specs=placed,
        out_specs=(
            P(("req", "kv"), None),
            P(None, ("req", "kv"), None),
            P(None, ("req", "kv"), None),
        ),
        check_vma=False,
    )
```

profile of v0, /device:TPU:1, one launch (start us, length us, event | category | flops | bytes accessed | tf_op | source)
XLA Modules:
  0.0 216.2 jit_solution(5172984267959892114)
XLA Ops:
  7.2 0.7 broadcast_add_fusion
  7.9 1.3 collective-permute-start.1
  9.2 1.1 copy.46
  10.3 1.3 collective-permute-start.2
  11.6 1.3 collective-permute-start
  12.9 1.4 reshape.106
  14.4 0.1 fusion.35
  14.5 1.0 collective-permute-done
  15.5 1.0 pad_maximum_fusion
  16.5 0.2 copy.44
  16.8 0.6 fusion.42
  17.4 0.3 fusion.29
  17.7 0.2 copy.50
  17.9 4.2 %all_to_all.76 = bf16[128,2,1024]{2,0,1:T(8,128)(2,1)S(1)} all-to-all(bf16[128,2,1024]{2,0,1:T(8,128)(2,1)S(1)} %copy.50), channel_id=1, replica_groups=mesh['req'=64,'kv'=2] {'kv'}, dimensions={1} | all-to-all | bytes 1048576 | tf_op jit(solution)/shard_map/all_to_all | solution.py:98
  22.1 6.4 %convolution_convert_fusion.1 = bf16[256,3584]{1,0:T(8,128)(2,1)} fusion(bf16[256,1024]{1,0:T(8,128)(2,1)S(1)} %bitcast.76, bf16[1024,3584]{1,0:T(8,128)(2,1)} %param.19), kind=kOutput, calls=%fused_computation.13 | convolution fusion | flops 1879965696 | bytes 9699328 | tf_op jit(solution)/shard_map/dot_general | solution.py:101
  28.6 0.6 copy-done
  29.2 2.5 %sort.31 = (s32[128]{0:T(128)}, s32[128]{0:T(128)S(1)}) sort(s32[128]{0:T(128)S(1)} %copy-done, s32[128]{0:T(128)S(1)} %iota.18), dimensions={0}, to_apply=%region_3.4 | sort | flops 896 | bytes 2048 | tf_op jit(solution)/shard_map/jit(argsort)/sort | solution.py:108
  31.8 1.2 gather_fusion.1
  33.0 0.7 copy.52
  33.8 10.9 %all-to-all-start.2 = ((s32[128,1,1]{2,1,0:T(1,128)}), s32[128,1,1]{2,1,0:T(1,128)S(1)}, u32[]{:S(2)}, u32[]{:S(2)}) async-start(s32[128,1,1]{2,1,0:T(1,128)} %copy.52), calls=%async_computation.3 | async-start | bytes 131072 | tf_op jit(solution)/shard_map/all_to_all | solution.py:51
  44.7 1.4 fusion.8
  46.2 1.8 fusion.12
  48.0 0.3 fusion.14
  48.3 1.1 gather_fusion.3
  49.4 0.5 broadcast.147
  49.9 1.2 reduce.1
  51.1 1.1 reshape.194
  52.2 2.0 all-to-all-done.2
  54.2 7.8 %all-to-all-start.3 = ((bf16[128,2,1792]{2,1,0:T(2,128)(2,1)}), bf16[128,2,1792]{2,1,0:T(2,128)(2,1)S(1)}, u32[]{:S(2)}, u32[]{:S(2)}) async-start(bf16[128,2,1792]{2,1,0:T(2,128)(2,1)} %reshape.194), calls=%async_computation.4 | async-start | bytes 1835008 | tf_op jit(solution)/shard_map/all_to_all | solution.py:50
  62.0 2.4 %reduce = s32[128]{0:T(128)S(1)} reduce(s32[128,1,1]{2,1,0:T(1,128)S(1)} %all-to-all-done.2, s32[]{:T(128)} %constant.17.clone.1), dimensions={1,2}, to_apply=%all_to_all.59.reduce_sub_computation | reduce | bytes 1028 | tf_op jit(solution)/shard_map/all_to_all | solution.py:51
  64.4 2.5 %sort.32 = (s32[128]{0:T(128)}, s32[128]{0:T(128)S(1)}) sort(s32[128]{0:T(128)S(1)} %reduce, s32[128]{0:T(128)S(1)} %iota.19), dimensions={0}, to_apply=%region_4.5 | sort | flops 896 | bytes 2048 | tf_op jit(solution)/shard_map/jit(argsort)/sort | solution.py:117
  67.0 13.0 %all-to-all-done.3 = bf16[128,2,1792]{2,1,0:T(2,128)(2,1)S(1)} async-done(((bf16[128,2,1792]{2,1,0:T(2,128)(2,1)}), bf16[128,2,1792]{2,1,0:T(2,128)(2,1)S(1)}, u32[]{:S(2)}, u32[]{:S(2)}) %all-to-all-start.3) | async-done | bytes 917536 | tf_op jit(solution)/shard_map/all_to_all | solution.py:50
  79.9 2.1 reshape.195
  82.0 1.6 copy.79
  83.7 2.0 gather_fusion.4
  85.7 0.2 reduce-scatter.5.cloned.1.call-start
  86.0 9.3 %all-gather.3.cloned.1.call-done = bf16[256,3584]{1,0:T(8,128)(2,1)} async-done(((bf16[128,3584]{1,0:T(8,128)(2,1)}), bf16[256,3584]{1,0:T(8,128)(2,1)}) %all-gather.3.cloned.1.call-update) | async-done | bytes 1835024 | tf_op jit(solution)/shard_map/all_gather | solution.py:119
  95.3 17.1 %fusion.43 = f32[256,3584]{1,0:T(8,128)} fusion(bf16[256,3584]{1,0:T(8,128)(2,1)} %all-gather.3.cloned.1.call-done, bf16[3584,3584]{1,0:T(8,128)(2,1)} %param.22), kind=kOutput, calls=%fused_computation.86 | convolution fusion | flops 6576668672 | bytes 31195136 | tf_op jit(solution)/shard_map/dot_general | solution.py:124
  112.4 24.6 %convolution_convert_fusion = bf16[256,3584]{1,0:T(8,128)(2,1)} fusion(bf16[3584,3584]{1,0:T(8,128)(2,1)} %param.24, bf16[256,3584]{1,0:T(8,128)(2,1)S(1)} %copy-done.7, bf16[3584,3584]{1,0:T(8,128)(2,1)} %param.23, f32[256,3584]{1,0:T(8,128)} %fusion.43), kind=kOutput, calls=%fused_computation.12 | convolution fusion | flops 13163429888 | bytes 58720256 | tf_op jit(solution)/shard_map/dot_general | solution.py:128
  137.0 0.9 copy-done.1
  137.9 0.9 gather_fusion.5
  138.8 0.7 reduce.4
  139.4 0.9 reshape.198
  140.3 9.2 %all-to-all-start.4 = ((bf16[128,2,512]{2,1,0:T(2,128)(2,1)}), bf16[128,2,512]{2,1,0:T(2,128)(2,1)S(1)}, u32[]{:S(2)}, u32[]{:S(2)}) async-start(bf16[128,2,512]{2,1,0:T(2,128)(2,1)} %reshape.198), calls=%async_computation.6 | async-start | bytes 524288 | tf_op jit(solution)/shard_map/all_to_all | solution.py:53
  149.5 0.9 gather_fusion.7
  150.4 0.7 reduce.3
  151.1 0.9 reshape.200
  152.0 8.7 %all-to-all-done.4 = bf16[128,2,512]{2,1,0:T(2,128)(2,1)S(1)} async-done(((bf16[128,2,512]{2,1,0:T(2,128)(2,1)}), bf16[128,2,512]{2,1,0:T(2,128)(2,1)S(1)}, u32[]{:S(2)}, u32[]{:S(2)}) %all-to-all-start.4) | async-done | bytes 262176 | tf_op jit(solution)/shard_map/all_to_all | solution.py:53
  160.6 4.4 %all-to-all-start.5 = ((bf16[128,2,512]{2,1,0:T(2,128)(2,1)}), bf16[128,2,512]{2,1,0:T(2,128)(2,1)S(1)}, u32[]{:S(2)}, u32[]{:S(2)}) async-start(bf16[128,2,512]{2,1,0:T(2,128)(2,1)} %reshape.200), calls=%async_computation.7 | async-start | bytes 524288 | tf_op jit(solution)/shard_map/all_to_all | solution.py:54
  165.0 1.1 gather_fusion
  166.2 1.2 reduce.2
  167.4 1.1 reshape.196
  168.5 7.6 %all-to-all-done.5 = bf16[128,2,512]{2,1,0:T(2,128)(2,1)S(1)} async-done(((bf16[128,2,512]{2,1,0:T(2,128)(2,1)}), bf16[128,2,512]{2,1,0:T(2,128)(2,1)S(1)}, u32[]{:S(2)}, u32[]{:S(2)}) %all-to-all-start.5) | async-done | bytes 262176 | tf_op jit(solution)/shard_map/all_to_all | solution.py:54
  176.1 5.1 %all-to-all-start.1 = ((bf16[128,2,1792]{2,1,0:T(2,128)(2,1)}), bf16[128,2,1792]{2,1,0:T(2,128)(2,1)}, u32[]{:S(2)}, u32[]{:S(2)}) async-start(bf16[128,2,1792]{2,1,0:T(2,128)(2,1)} %reshape.196), calls=%async_computation.2 | async-start | bytes 1835008 | tf_op jit(solution)/shard_map/all_to_all | solution.py:52
  181.3 0.2 reshape.199
  181.6 0.9 gather_fusion.6
  182.5 0.2 reshape.201
  182.8 0.9 gather_fusion.8
  183.7 0.8 bitcast_bitcast_fusion
  184.5 14.5 %all-to-all-done.1 = bf16[128,2,1792]{2,1,0:T(2,128)(2,1)} async-done(((bf16[128,2,1792]{2,1,0:T(2,128)(2,1)}), bf16[128,2,1792]{2,1,0:T(2,128)(2,1)}, u32[]{:S(2)}, u32[]{:S(2)}) %all-to-all-start.1) | async-done | bytes 917536 | tf_op jit(solution)/shard_map/all_to_all | solution.py:52
  199.0 5.4 %reshape.197 = bf16[128,1,3584]{2,1,0:T(2,128)(2,1)S(1)} reshape(bf16[128,2,1792]{2,1,0:T(2,128)(2,1)} %all-to-all-done.1) | data formatting | bytes 1835008
  204.6 1.1 gather_fusion.2
  205.7 1.4 fusion.15
  207.2 2.5 %fusion.18 = bf16[128,3584]{1,0:T(8,128)(2,1)} fusion(bf16[128,3584]{1,0:T(8,128)(2,1)} %reduce-scatter.5.cloned.1.call-done, bf16[128,3584]{1,0:T(8,128)(2,1)S(1)} %gather_fusion.2, f32[3584]{0:T(1024)S(1)} %copy-done.6, f32[128]{0:T(128)S(1)} %add_rsqrt_fusion), kind=kLoop, calls=%fused_computation.37 | loop fusion | flops 2752512 | bytes 2767360 | tf_op jit(solution)/shard_map/convert_element_type | solution.py:133
  (41 shorter events, 0.6 us)
Async XLA Ops:
  7.2 37.5 %reduce-scatter.3.cloned.1.call-start = ((), (), s32[]{:S(2)}) async-start(), calls=%async_computation.8 | async-start | bytes 2752512 | tf_op jit(solution)/shard_map/reduce_scatter | solution.py:100
  7.9 6.5 %collective-permute-start.1 = (s32[128]{0:T(128)S(1)}, s32[128]{0:T(128)S(1)}, u32[]{:S(2)}, u32[]{:S(2)}) collective-permute-start(s32[128]{0:T(128)S(1)} %broadcast_add_fusion), channel_id=1, source_target_pairs={{0,1},{2,3},{4,5},{6,7},{8,9},{10,11},{12,13},{14,15},{16,17},{18,... | collective-permute-start | bytes 1544 | tf_op jit(solution)/shard_map/ppermute | solution.py:19
  10.3 6.4 %collective-permute-start.2 = (bf16[128,1024]{0,1:T(8,128)(2,1)S(1)}, bf16[128,1024]{0,1:T(8,128)(2,1)S(1)}, u32[]{:S(2)}, u32[]{:S(2)}) collective-permute-start(bf16[128,1024]{0,1:T(8,128)(2,1)S(1)} %copy.46), channel_id=1, source_target_pairs={{0,1},{2,3},{4,5},{6,7},{8,9},{10,11},{12,13},{14,15},{16,17},{18,... | collective-permute-start | bytes 786440 | tf_op jit(solution)/shard_map/ppermute | solution.py:19
  11.6 4.0 %collective-permute-start = (bf16[128,1024]{1,0:T(8,128)(2,1)}, bf16[128,1024]{1,0:T(8,128)(2,1)S(1)}, u32[]{:S(2)}, u32[]{:S(2)}) collective-permute-start(bf16[128,1024]{1,0:T(8,128)(2,1)} %param.15), channel_id=1, source_target_pairs={{0,1},{2,3},{4,5},{6,7},{8,9},{10,11},{12,13},{14,15},{16,17},{18,... | collective-permute-start | bytes 786440 | tf_op jit(solution)/shard_map/ppermute | solution.py:19
  28.6 0.7 copy-start
  28.6 17.6 %copy-start.3 = (bf16[128,3584]{1,0:T(8,128)(2,1)S(1)}, bf16[128,3584]{1,0:T(8,128)(2,1)}, u32[]{:S(2)}) copy-start(bf16[128,3584]{1,0:T(8,128)(2,1)} %param.16) | copy-start | bytes 2752516
  28.6 17.6 %copy-start.4 = (f32[3584]{0:T(1024)S(1)}, f32[3584]{0:T(1024)}, u32[]{:S(2)}) copy-start(f32[3584]{0:T(1024)} %param.20) | copy-start | bytes 43012
  33.8 20.4 %all-to-all-start.2 = ((s32[128,1,1]{2,1,0:T(1,128)}), s32[128,1,1]{2,1,0:T(1,128)S(1)}, u32[]{:S(2)}, u32[]{:S(2)}) async-start(s32[128,1,1]{2,1,0:T(1,128)} %copy.52), calls=%async_computation.3 | async-start | bytes 131072 | tf_op jit(solution)/shard_map/all_to_all | solution.py:51
  44.7 3.3 %copy-start.5 = (f32[3584]{0:T(1024)S(1)}, f32[3584]{0:T(1024)}, u32[]{:S(2)}) copy-start(f32[3584]{0:T(1024)} %param.21) | copy-start | bytes 43012
  54.2 25.7 %all-to-all-start.3 = ((bf16[128,2,1792]{2,1,0:T(2,128)(2,1)}), bf16[128,2,1792]{2,1,0:T(2,128)(2,1)S(1)}, u32[]{:S(2)}, u32[]{:S(2)}) async-start(bf16[128,2,1792]{2,1,0:T(2,128)(2,1)} %reshape.194), calls=%async_computation.4 | async-start | bytes 1835008 | tf_op jit(solution)/shard_map/all_to_all | solution.py:50
  62.0 33.3 %all-gather.3.cloned.1.call-start = ((), (), s32[]{:S(2)}) async-start(), calls=%async_computation.10 | async-start | bytes 2752512 | tf_op jit(solution)/shard_map/all_gather | solution.py:119
  85.7 120.0 %reduce-scatter.5.cloned.1.call-start = ((), (), s32[]{:S(2)}) async-start(), calls=%async_computation.9 | async-start | bytes 2752512 | tf_op jit(solution)/shard_map/reduce_scatter | solution.py:127
  95.3 17.1 %copy-start.7 = (bf16[256,3584]{1,0:T(8,128)(2,1)S(1)}, bf16[256,3584]{1,0:T(8,128)(2,1)}, u32[]{:S(2)}) copy-start(bf16[256,3584]{1,0:T(8,128)(2,1)} %all-gather.3.cloned.1.call-done) | copy-start | bytes 5505028
  136.9 0.9 copy-start.1
  137.9 11.6 %copy-start.2 = (bf16[128,1024]{1,0:T(8,128)(2,1)S(1)}, bf16[128,1024]{1,0:T(8,128)(2,1)}, u32[]{:S(2)}) copy-start(bf16[128,1024]{1,0:T(8,128)(2,1)} %param.15) | copy-start | bytes 786436
  140.3 20.3 %all-to-all-start.4 = ((bf16[128,2,512]{2,1,0:T(2,128)(2,1)}), bf16[128,2,512]{2,1,0:T(2,128)(2,1)S(1)}, u32[]{:S(2)}, u32[]{:S(2)}) async-start(bf16[128,2,512]{2,1,0:T(2,128)(2,1)} %reshape.198), calls=%async_computation.6 | async-start | bytes 524288 | tf_op jit(solution)/shard_map/all_to_all | solution.py:53
  160.6 15.5 %all-to-all-start.5 = ((bf16[128,2,512]{2,1,0:T(2,128)(2,1)}), bf16[128,2,512]{2,1,0:T(2,128)(2,1)S(1)}, u32[]{:S(2)}, u32[]{:S(2)}) async-start(bf16[128,2,512]{2,1,0:T(2,128)(2,1)} %reshape.200), calls=%async_computation.7 | async-start | bytes 524288 | tf_op jit(solution)/shard_map/all_to_all | solution.py:54
  176.1 22.9 %all-to-all-start.1 = ((bf16[128,2,1792]{2,1,0:T(2,128)(2,1)}), bf16[128,2,1792]{2,1,0:T(2,128)(2,1)}, u32[]{:S(2)}, u32[]{:S(2)}) async-start(bf16[128,2,1792]{2,1,0:T(2,128)(2,1)} %reshape.196), calls=%async_computation.2 | async-start | bytes 1835008 | tf_op jit(solution)/shard_map/all_to_all | solution.py:52
  204.6 2.6 %copy-start.6 = (f32[3584]{0:T(1024)S(1)}, f32[3584]{0:T(1024)}, u32[]{:S(2)}) copy-start(f32[3584]{0:T(1024)} %param.25) | copy-start | bytes 43012
Sparse Core Ops, SparseCore 0:
  28.7 15.0 reduce-scatter.2
  85.9 9.4 all-gather.2
  137.1 13.3 reduce-scatter.4
where the time goes:
time: 217 us; the launch traced here: 216 us
  waiting for transfers between devices  56.2 us (26%)
  matrix products  48.9 us (23%)
  starting transfers between devices  41.6 us (19%)
  local copies, waits for them, and re-layouts  30.5 us (14%)
  other arithmetic  20.6 us (9%)
  between operations  14.1 us (6%)
  blocking collectives  4.22 us (2%)
    dot_general x1, matrix products, per_device(): jnp.dot(active, down_weight, preferred_element_type=jnp.float32)  24.6 us
    dot_general x1, matrix products, per_device(): gate_part = jnp.dot(picked, gate_weight, preferred_element_type=jnp.float32)  17.1 us
    unnamed x29, local copies, waits for them, and re-layouts  16.6 us
    all_to_all x1, waiting for transfers between devices, send_rows(): lax.all_to_all(stream_part, ('req', 'kv'), split_axis=0, concat_axis=0, t...  14.5 us
    all_to_all x1, waiting for transfers between devices, send_rows(): lax.all_to_all(normed_part, ('req', 'kv'), split_axis=0, concat_axis=0, t...  13 us
    all_to_all x1, starting transfers between devices, send_rows(): lax.all_to_all(normed_pos, ('req', 'kv'), split_axis=0, concat_axis=0, ti...  10.9 us
    all_gather x1, waiting for transfers between devices, per_device(): group_normed = lax.all_gather(own_normed, 'kv', axis=0, tiled=True)  9.35 us
    all_to_all x1, starting transfers between devices, send_rows(): lax.all_to_all(key_portion, ('req', 'kv'), split_axis=0, concat_axis=0, t...  9.19 us
  transfers between devices with their start and end apart: 11, of which 7 were waited for; matrix products, arithmetic and copies ran while one was open for 18% of the time, Pallas kernels for 0%

commit v1 on v0

v1 whole, which is shorter than its diff:
```python
import jax
import jax.numpy as jnp
from jax import lax
from jax.experimental import pallas as pl
from jax.experimental.pallas import tpu as pltpu
from jax.sharding import PartitionSpec as P

MESH = pl.DeviceIdType.MESH
CHIPS = 64
SIDE = 4
ROWS = 128
WIDTH = 3584
HEAD = 256
OWN_HEADS = 4
HALF = 1024
KV_HALF = 512
KV_WIDTH = 2048
CHUNK = 512
CHUNKS = WIDTH // CHUNK
SLOTS = 10
GROUPS = 8
PER_GROUP = CHIPS // GROUPS
CAP = 50.0
EPS = 1e-06
BF = jnp.bfloat16
F32 = jnp.float32


def cols(j, width=CHUNK):
    return pl.ds(pl.multiple_of(j * width, width), width)


def rows_of(core):
    return pl.ds(pl.multiple_of(core * ROWS, ROWS), ROWS)


def kernel(
    q, k, v, res, seg, rg, ow, ag, pg, gw, uw, dw, og,
    lo, kc, vc,
    wbuf, qb, kb, vb, segb, kvl, rgb, gains, rb, att, part, prec, pkv, kvr, pks, strr,
    pb, xb, act, drec, kvo, pf,
    in_sem, o_sem, w_sem, out_sem, ex_send, ex_recv, pr_send, pr_recv, dn_send, dn_recv,
    kv_send, kv_recv, kvf_send, kvf_recv, st_send, st_recv, stf_send, stf_recv,
):
    chip = lax.axis_index("req")
    core = lax.axis_index("kv")
    other = 1 - core
    sibling = (chip, other)
    z, y, x = lax.div(chip, 16), lax.rem(lax.div(chip, 4), 4), lax.rem(chip, 4)

    def chip_at(i):
        zz = lax.rem(z + lax.div(i, 16), 4)
        yy = lax.rem(y + lax.rem(lax.div(i, 4), 4), 4)
        xx = lax.rem(x + lax.rem(i, 4), 4)
        return zz * 16 + yy * 4 + xx

    def local(src, dst, sem):
        return pltpu.make_async_copy(src, dst, sem)

    def remote(src, dst, send, recv, device):
        return pltpu.make_async_remote_copy(
            src_ref=src, dst_ref=dst, send_sem=send, recv_sem=recv, device_id=device, device_id_type=MESH
        )

    barrier = pltpu.get_barrier_semaphore()
    pl.semaphore_signal(barrier, inc=1, device_id=sibling, device_id_type=MESH)

    def greet(i, c):
        pl.semaphore_signal(barrier, inc=1, device_id=(chip_at(i), core), device_id_type=MESH)
        return c

    lax.fori_loop(1, CHIPS, greet, 0)

    ins = [
        local(rg, rgb, in_sem.at[0]),
        local(k, kvl.at[:, pl.ds(0, HALF)], in_sem.at[1]),
        local(v, kvl.at[:, pl.ds(HALF, HALF)], in_sem.at[2]),
        local(seg, segb.at[core], in_sem.at[3]),
        local(q.at[:, cols(core, HALF)], qb.at[rows_of(core), :], in_sem.at[4]),
        local(k.at[:, cols(core, KV_HALF)], kb.at[rows_of(core), :], in_sem.at[5]),
        local(v.at[:, cols(core, KV_HALF)], vb.at[rows_of(core), :], in_sem.at[6]),
        local(ag, gains.at[0], in_sem.at[7]),
        local(pg, gains.at[1], in_sem.at[8]),
        local(og, gains.at[2], in_sem.at[9]),
        local(res, rb, in_sem.at[10]),
    ]
    for c in ins:
        c.start()

    def o_load(j):
        return local(ow.at[:, cols(j)], wbuf.at[pl.ds(pl.multiple_of(j * HALF, HALF), HALF), :], o_sem.at[j])

    for j in range(CHUNKS):
        o_load(j).start()

    def w_load(src, j, unit):
        slot = lax.rem(unit, SLOTS) if not isinstance(unit, int) else unit % SLOTS
        return local(
            src.at[:, cols(j)],
            wbuf.at[pl.ds(pl.multiple_of(slot * WIDTH, WIDTH), WIDTH), :],
            w_sem.at[slot],
        )

    for c in ins[:3]:
        c.wait()
    to = rgb[...]
    pick = lax.broadcasted_iota(jnp.int32, (ROWS, ROWS), 0) == lax.shift_right_logical(to, 7)
    pos = jnp.sum(
        jnp.where(pick, jnp.bitwise_and(to, 255).astype(F32), 0.0), axis=1, keepdims=True
    )
    pick = pick.astype(BF)
    pkv[:, :, KV_WIDTH:] = jnp.broadcast_to(pos, (ROWS, ROWS)).astype(BF).reshape(CHIPS, 2, ROWS)
    for j in range(KV_WIDTH // CHUNK):
        y_rows = jnp.dot(pick, kvl[:, cols(j)], preferred_element_type=F32).astype(BF)
        pkv[:, :, cols(j)] = y_rows.reshape(CHIPS, 2, CHUNK)

    pl.semaphore_wait(barrier, CHIPS)

    exchange = [
        remote(seg, segb.at[core], ex_send.at[0], ex_recv.at[0], sibling),
        remote(
            q.at[:, cols(other, HALF)], qb.at[rows_of(core), :], ex_send.at[1], ex_recv.at[1], sibling
        ),
        remote(
            k.at[:, cols(other, KV_HALF)], kb.at[rows_of(core), :], ex_send.at[2], ex_recv.at[2], sibling
        ),
        remote(
            v.at[:, cols(other, KV_HALF)], vb.at[rows_of(core), :], ex_send.at[3], ex_recv.at[3], sibling
        ),
    ]
    for c in exchange:
        c.start()

    def scatter(packets, landing, send, recv):
        here = local(packets.at[chip], landing.at[core, 0], recv.at[0])
        here.start()

        def one(i, c):
            there = chip_at(i)
            remote(
                packets.at[there], landing.at[core, i], send, recv.at[lax.div(i, PER_GROUP)], (there, core)
            ).start()
            return c

        lax.fori_loop(1, CHIPS, one, 0)

    def scattered(packets, landing, send, recv):
        remote(
            packets.at[pl.ds(0, CHIPS - 1)], landing.at[core, pl.ds(0, CHIPS - 1)], send, recv.at[0], sibling
        ).wait_send()

    def group(i):
        return pl.ds(i * PER_GROUP, PER_GROUP)

    def forward(landing, i, send, recv):
        return remote(
            landing.at[core, group(i)], landing.at[core, group(i)], send.at[i], recv.at[i], sibling
        )

    def hand_on(landing, recv, send_f, recv_f):
        def one(i, c):
            block = landing.at[core, group(i)]
            local(block, block, recv.at[i]).wait()
            forward(landing, i, send_f, recv_f).start()
            return c

        lax.fori_loop(0, GROUPS, one, 0)

        def arrived(i, c):
            theirs = landing.at[other, group(i)]
            remote(theirs, theirs, send_f.at[i], recv_f.at[i], sibling).wait_recv()
            return c

        lax.fori_loop(0, GROUPS, arrived, 0)

    scatter(pkv, kvr, kv_send, kv_recv)

    for unit in range(2, SLOTS):
        w_load(gw if unit % 2 == 0 else uw, (unit - 2) // 2, unit).start()

    for c in ins[3:]:
        c.wait()
    for c in exchange:
        c.wait_recv()
    two = 2 * ROWS
    t_at = lax.broadcasted_iota(jnp.int32, (two, two), 0)
    s_at = lax.broadcasted_iota(jnp.int32, (two, two), 1)
    last = jnp.concatenate([segb[0], segb[1]], axis=1) - chip * two
    allowed = (s_at <= t_at) & (last >= t_at)
    for h in range(OWN_HEADS):
        own = pl.ds(h * HEAD, HEAD)
        key = pl.ds(h // 2 * HEAD, HEAD)
        raw = lax.dot_general(
            qb[:, own], kb[:, key], (((1,), (1,)), ((), ())), preferred_element_type=F32
        )
        scores = CAP * jnp.tanh(raw * (HEAD**-0.5 / CAP))
        probs = jnp.where(allowed, jnp.exp(scores), 0.0)
        totals = jnp.sum(probs, axis=-1, keepdims=True)
        mixed = jnp.dot(probs.astype(BF), vb[:, key], preferred_element_type=F32)
        att[:, own] = (mixed * (1.0 / totals)).astype(BF)

    def halves(landing, j, send, recv):
        return remote(
            part.at[rows_of(other), cols(j)], landing.at[:, cols(j)], send.at[j], recv.at[j], sibling
        )

    def project(j, c):
        o_load(j).wait()
        w = wbuf[pl.ds(pl.multiple_of(j * HALF, HALF), HALF), :]
        part[:, cols(j)] = jnp.dot(att[...], w, preferred_element_type=F32).astype(BF)
        halves(prec, j, pr_send, pr_recv).start()
        return c

    lax.fori_loop(0, CHUNKS, project, 0)
    w_load(gw, 4, SLOTS).start()
    w_load(uw, 4, SLOTS + 1).start()

    def lanes_sum(value):
        total = value[:, 0:128]
        for i in range(1, CHUNK // 128):
            total = total + value[:, i * 128 : (i + 1) * 128]
        return total

    def sum_halves(landing, send, recv):
        def one(j, squares):
            halves(landing, j, send, recv).wait_recv()
            both = part[rows_of(core), cols(j)].astype(F32) + landing[:, cols(j)].astype(F32)
            pf[:, cols(j)] = both
            return squares + lanes_sum(both * both)

        squares = lax.fori_loop(0, CHUNKS, one, jnp.zeros((ROWS, 128), F32))
        return lax.rsqrt(jnp.sum(squares, axis=-1, keepdims=True) * (1.0 / WIDTH) + EPS)

    scale = sum_halves(prec, pr_send, pr_recv)

    def to_packets(j, c):
        stream = (rb[:, cols(j)].astype(F32) + pf[:, cols(j)] * scale * gains[0, :, cols(j)]).astype(BF)
        y_rows = jnp.dot(pick, stream, preferred_element_type=F32).astype(BF)
        pks[:, :, cols(j)] = y_rows.reshape(CHIPS, 2, CHUNK)
        return c

    lax.fori_loop(0, CHUNKS, to_packets, 0)
    scatter(pks, strr, st_send, st_recv)

    hand_on(kvr, kv_recv, kvf_send, kvf_recv)
    at = kvr[:, :, :, KV_WIDTH:].reshape(two, 128).astype(F32)
    at = jnp.transpose(at)[0:1, :].astype(jnp.int32)
    place = (t_at == at).astype(BF)
    own_place = (t_at[0:ROWS, :] + core * ROWS == at).astype(BF)
    for j in range(KV_WIDTH // CHUNK):
        got = jnp.dot(
            own_place, kvr[:, :, :, cols(j)].reshape(two, CHUNK), preferred_element_type=F32
        ).astype(BF)
        kvo[2 * j] = got[:, 0:HEAD]
        kvo[2 * j + 1] = got[:, HEAD:]
    outs = [
        local(kvo.at[pl.ds(0, 4)], kc, out_sem.at[0]),
        local(kvo.at[pl.ds(4, 4)], vc, out_sem.at[1]),
    ]
    for c in outs:
        c.start()

    hand_on(strr, st_recv, stf_send, stf_recv)

    def put(j, squares):
        got = jnp.dot(
            place, strr[:, :, :, cols(j)].reshape(two, CHUNK), preferred_element_type=F32
        )
        pb[:, cols(j)] = got.astype(BF)
        return squares + lanes_sum(got * got)

    squares = lax.fori_loop(0, CHUNKS, put, jnp.zeros((two, 128), F32))
    scale = lax.rsqrt(jnp.sum(squares, axis=-1, keepdims=True) * (1.0 / WIDTH) + EPS)

    def norm(j, c):
        xb[:, cols(j)] = (pb[:, cols(j)].astype(F32) * scale * gains[1, :, cols(j)]).astype(BF)
        return c

    lax.fori_loop(0, CHUNKS, norm, 0)

    def weight(unit, i):
        slot = lax.rem(unit, SLOTS)
        return wbuf[
            pl.ds(pl.multiple_of(slot * WIDTH, WIDTH), WIDTH), pl.ds(i * 256, 256)
        ]

    def loaded(unit):
        slot = lax.rem(unit, SLOTS)
        block = wbuf.at[pl.ds(pl.multiple_of(slot * WIDTH, WIDTH), WIDTH), :]
        local(block, block, w_sem.at[slot]).wait()

    def hidden(j, c):
        loaded(2 + 2 * j)
        loaded(3 + 2 * j)
        for i in range(CHUNK // 256):
            u = jnp.dot(xb[...], weight(2 + 2 * j, i), preferred_element_type=F32)
            up = jnp.dot(xb[...], weight(3 + 2 * j, i), preferred_element_type=F32)
            gelu = 0.5 * u * (1.0 + jnp.tanh(0.7978845608028654 * (u + 0.044715 * (u * u * u))))
            act[:, pl.ds(pl.multiple_of(j * CHUNK + i * 256, 256), 256)] = (gelu * up).astype(BF)

        @pl.when(j < 2)
        def _():
            w_load(gw, 5 + j, 12 + 2 * j).start()
            w_load(uw, 5 + j, 13 + 2 * j).start()

        @pl.when((j >= 2) & (j < 6))
        def _():
            w_load(dw, 2 * (j - 2), 12 + 2 * j).start()

        @pl.when((j >= 2) & (j < 5))
        def _():
            w_load(dw, 2 * (j - 2) + 1, 13 + 2 * j).start()

        return c

    lax.fori_loop(0, CHUNKS, hidden, 0)

    def projected(j, c):
        halves(prec, j, pr_send, pr_recv).wait_send()
        return c

    lax.fori_loop(0, CHUNKS, projected, 0)

    def down(j, c):
        loaded(16 + j)
        for i in range(CHUNK // 256):
            got = jnp.dot(act[...], weight(16 + j, i), preferred_element_type=F32)
            part[:, pl.ds(pl.multiple_of(j * CHUNK + i * 256, 256), 256)] = got.astype(BF)
        halves(drec, j, dn_send, dn_recv).start()
        return c

    lax.fori_loop(0, CHUNKS, down, 0)
    scale = sum_halves(drec, dn_send, dn_recv)

    def finish(j, c):
        rb[:, cols(j)] = (
            pb[rows_of(core), cols(j)].astype(F32) + pf[:, cols(j)] * scale * gains[2, :, cols(j)]
        ).astype(BF)
        return c

    lax.fori_loop(0, CHUNKS, finish, 0)
    last_out = local(rb, lo, out_sem.at[2])
    last_out.start()

    for c in exchange:
        c.wait_send()
    scattered(pkv, kvr, kv_send, kv_recv)
    scattered(pks, strr, st_send, st_recv)

    def sent(i, c):
        forward(kvr, i, kvf_send, kvf_recv).wait_send()
        forward(strr, i, stf_send, stf_recv).wait_send()
        return c

    lax.fori_loop(0, GROUPS, sent, 0)

    def down_sent(j, c):
        halves(drec, j, dn_send, dn_recv).wait_send()
        return c

    lax.fori_loop(0, CHUNKS, down_sent, 0)
    for c in outs:
        c.wait()
    last_out.wait()


def per_device(
    queries,
    keys,
    values,
    residual,
    segment_ids,
    regroup,
    out_weight,
    attn_gain,
    pre_gain,
    gate_weight,
    up_weight,
    down_weight,
    post_gain,
):
    dma = pltpu.SemaphoreType.DMA
    vmem = pltpu.VMEM
    return pl.pallas_call(
        kernel,
        out_shape=(
            jax.ShapeDtypeStruct((ROWS, WIDTH), BF),
            jax.ShapeDtypeStruct((4, ROWS, HEAD), BF),
            jax.ShapeDtypeStruct((4, ROWS, HEAD), BF),
        ),
        in_specs=[pl.BlockSpec(memory_space=pl.ANY)] * 13,
        out_specs=(pl.BlockSpec(memory_space=pl.ANY),) * 3,
        scratch_shapes=[
            vmem((SLOTS * WIDTH, CHUNK), BF),
            vmem((2 * ROWS, HALF), BF),
            vmem((2 * ROWS, KV_HALF), BF),
            vmem((2 * ROWS, KV_HALF), BF),
            vmem((2, 1, ROWS), jnp.int32),
            vmem((ROWS, KV_WIDTH), BF),
            vmem((1, ROWS), jnp.int32),
            vmem((3, 1, WIDTH), F32),
            vmem((ROWS, WIDTH), BF),
            vmem((2 * ROWS, HALF), BF),
            vmem((2 * ROWS, WIDTH), BF),
            vmem((ROWS, WIDTH), BF),
            vmem((CHIPS, 2, KV_WIDTH + 128), BF),
            vmem((2, CHIPS, 2, KV_WIDTH + 128), BF),
            vmem((CHIPS, 2, WIDTH), BF),
            vmem((2, CHIPS, 2, WIDTH), BF),
            vmem((2 * ROWS, WIDTH), BF),
            vmem((2 * ROWS, WIDTH), BF),
            vmem((2 * ROWS, WIDTH), BF),
            vmem((ROWS, WIDTH), BF),
            vmem((8, ROWS, HEAD), BF),
            vmem((ROWS, WIDTH), F32),
            dma((11,)),
            dma((CHUNKS,)),
            dma((SLOTS,)),
            dma((3,)),
            dma((4,)),
            dma((4,)),
            dma((CHUNKS,)),
            dma((CHUNKS,)),
            dma((CHUNKS,)),
            dma((CHUNKS,)),
            dma,
            dma((GROUPS,)),
            dma((GROUPS,)),
            dma((GROUPS,)),
            dma,
            dma((GROUPS,)),
            dma((GROUPS,)),
            dma((GROUPS,)),
        ],
        compiler_params=pltpu.CompilerParams(
            collective_id=0, has_side_effects=True, vmem_limit_bytes=62 * 1024 * 1024
        ),
        name="layer",
    )(
        queries,
        keys,
        values,
        residual,
        segment_ids.reshape(1, ROWS),
        regroup.reshape(1, ROWS),
        out_weight,
        attn_gain.reshape(1, WIDTH),
        pre_gain.reshape(1, WIDTH),
        gate_weight,
        up_weight,
        down_weight,
        post_gain.reshape(1, WIDTH),
    )


def solution(mesh):
    rows = P(("req", "kv"), None)
    flat = P(("req", "kv"))
    return jax.shard_map(
        per_device,
        mesh=mesh,
        in_specs=(
            rows, rows, rows, rows, flat, flat, P("kv", None), P(), P(),
            P(None, "kv"), P(None, "kv"), P("kv", None), P(),
        ),
        out_specs=(rows, P(None, ("req", "kv"), None), P(None, ("req", "kv"), None)),
        check_vma=False,
    )
```

time: 217 us -> 74 us (0.34)
  Pallas kernels: 0 us -> 63.5 us
  waiting for transfers between devices: 56.2 us -> 0 us
  matrix products: 48.9 us -> 0 us
  starting transfers between devices: 41.6 us -> 0 us
  local copies, waits for them, and re-layouts: 30.5 us -> 9.48 us
  other arithmetic: 20.6 us -> 0 us
  between operations: 14.1 us -> 0.64 us
  blocking collectives: 4.22 us -> 0 us
    pallas_call x0 -> x1, Pallas kernels: none -> 63.5 us  [per_device(): pl.pallas_call(kernel, out_shape=(jax.ShapeDtypeStruct((ROWS, WIDTH), BF)...]
    dot_general x5 -> x0, matrix products: 48.9 us -> none  [the longest x1 24.6 us: per_device(): jnp.dot(active, down_weight, preferred_element_type=jnp.float32)]
    all_to_all x5 -> x0, waiting for transfers between devices: 45.8 us -> none  [the longest x1 14.5 us: send_rows(): lax.all_to_all(stream_part, ('req', 'kv'), split_axis=0, concat_axis=0, t...]
    all_to_all x5 -> x0, starting transfers between devices: 37.4 us -> none  [the longest x1 10.9 us: send_rows(): lax.all_to_all(normed_pos, ('req', 'kv'), split_axis=0, concat_axis=0, ti...]
    unnamed x29 -> x3, local copies, waits for them, and re-layouts: 16.6 us -> 5.5 us
    gather x9 -> x0, local copies, waits for them, and re-layouts: 10.1 us -> none  [the longest x1 2.05 us: per_device(): own_normed = received[0][placed]]
    all_gather x1 -> x0, waiting for transfers between devices: 9.35 us -> none  [per_device(): group_normed = lax.all_gather(own_normed, 'kv', axis=0, tiled=True)]
    all_to_all x5 -> x0, other arithmetic: 6.14 us -> none  [the longest x1 2.35 us: send_rows(): lax.all_to_all(normed_pos, ('req', 'kv'), split_axis=0, concat_axis=0, ti...]
  transfers between devices with their start and end apart: 11 -> 0, of which waited for: 7 -> 0; matrix products, arithmetic and copies ran while one was open for 18% -> 0% of each run, Pallas kernels for 0% -> 0%
where the time goes in v1:
time: 74 us; the launch traced here: 73.6 us
  Pallas kernels  63.5 us (86%)
  local copies, waits for them, and re-layouts  9.48 us (13%)
    pallas_call x1, Pallas kernels, per_device(): pl.pallas_call(kernel, out_shape=(jax.ShapeDtypeStruct((ROWS, WIDTH), BF)...  63.5 us
    unnamed x3, local copies, waits for them, and re-layouts  5.5 us

profile of v1, /device:TPU:1, one launch (start us, length us, event | category | flops | bytes accessed | tf_op | source)
XLA Modules:
  0.0 73.6 jit_solution(3890195536025825256)
XLA Ops:
  0.6 1.3 %reshape.23.ag = f32[1,3584]{1,0:T(1,128)} reshape(f32[3584]{0:T(1024)} %param.20) | data formatting | bytes 28672 | tf_op jit(solution)/shard_map/reshape | solution.py:447
  2.0 1.3 %reshape.24.pg = f32[1,3584]{1,0:T(1,128)} reshape(f32[3584]{0:T(1024)} %param.21) | data formatting | bytes 28672 | tf_op jit(solution)/shard_map/reshape | solution.py:448
  3.3 1.3 %reshape.25.og = f32[1,3584]{1,0:T(1,128)} reshape(f32[3584]{0:T(1024)} %param.25) | data formatting | bytes 28672 | tf_op jit(solution)/shard_map/reshape | solution.py:452
  4.6 63.5 %layer.1 = (bf16[128,3584]{1,0:T(8,128)(2,1)}, bf16[4,128,256]{2,1,0:T(8,128)(2,1)}, bf16[4,128,256]{2,1,0:T(8,128)(2,1)}) custom-call(bf16[128,2048]{1,0:T(8,128)(2,1)} %q.1, bf16[128,1024]{1,0:T(8,128)(2,1)} %k.1, bf16[128,1024]{1,0:T(8,128)(2,1)} %v.1, bf16[128,3584]{1,0:T(8,128)(2,1)} %res.1, s32[1,128]{1,0:T(1,128)} %bitcast.2, s32[1,128]{1,0:T(1,128)} %bitcast.3, ...), custom_call_target="tpu_custom_call" | custom-call | tf_op jit(solution)/shard_map/layer/pallas_call | solution.py:384
  68.1 2.2 %copy.19 = bf16[128,3584]{1,0:T(8,128)(2,1)} copy(bf16[128,3584]{1,0:T(8,128)(2,1)} %get-tuple-element.6) | data formatting | bytes 1835008
  70.3 1.7 %copy.20 = bf16[4,128,256]{2,1,0:T(8,128)(2,1)} copy(bf16[4,128,256]{2,1,0:T(8,128)(2,1)} %get-tuple-element.7) | data formatting | bytes 524288
  72.0 1.7 %copy.21 = bf16[4,128,256]{2,1,0:T(8,128)(2,1)} copy(bf16[4,128,256]{2,1,0:T(8,128)(2,1)} %get-tuple-element.8) | data formatting | bytes 524288

commit v2 on v1

--- a/solution.py
+++ b/solution.py
@@ -27,6 +27,8 @@
 
 
 def cols(j, width=CHUNK):
+    if isinstance(j, int):
+        return pl.ds(j * width, width)
     return pl.ds(pl.multiple_of(j * width, width), width)
 
 
@@ -34,25 +36,53 @@
     return pl.ds(pl.multiple_of(core * ROWS, ROWS), ROWS)
 
 
+def lanes_sum(value):
+    total = value[:, 0:128]
+    for i in range(1, CHUNK // 128):
+        total = total + value[:, i * 128 : (i + 1) * 128]
+    return total
+
+
 def kernel(
-    q, k, v, res, seg, rg, ow, ag, pg, gw, uw, dw, og,
-    lo, kc, vc,
-    wbuf, qb, kb, vb, segb, kvl, rgb, gains, rb, att, part, prec, pkv, kvr, pks, strr,
-    pb, xb, act, drec, kvo, pf,
-    in_sem, o_sem, w_sem, out_sem, ex_send, ex_recv, pr_send, pr_recv, dn_send, dn_recv,
+    q, k, v, res, seg, rg, ow, ag, pg, gw, uw, dw,
+    mine, theirs, own_rows, kvo,
+    wbuf, qb, kb, vb, segb, kvl, rgb, ag_row, pg_row, rb, att, part, prec, pkv, kvr, pks, strr,
+    pb, xb, act, kvb, pf,
+    in_sem, o_sem, w_sem, out_sem, keep_sem, ex_send, ex_recv, pr_send, pr_recv, dn_send, dn_recv,
     kv_send, kv_recv, kvf_send, kvf_recv, st_send, st_recv, stf_send, stf_recv,
 ):
     chip = lax.axis_index("req")
     core = lax.axis_index("kv")
     other = 1 - core
     sibling = (chip, other)
-    z, y, x = lax.div(chip, 16), lax.rem(lax.div(chip, 4), 4), lax.rem(chip, 4)
-
-    def chip_at(i):
-        zz = lax.rem(z + lax.div(i, 16), 4)
-        yy = lax.rem(y + lax.rem(lax.div(i, 4), 4), 4)
-        xx = lax.rem(x + lax.rem(i, 4), 4)
-        return zz * 16 + yy * 4 + xx
+    z = lax.div(chip, SIDE * SIDE)
+    plane = chip - z * (SIDE * SIDE)
+    y = lax.div(plane, SIDE)
+    x = plane - y * SIDE
+
+    def wrap(at):
+        return jnp.where(at >= SIDE, at - SIDE, at)
+
+    across = [wrap(x + n) for n in range(SIDE)]
+
+    def each_chip(do):
+        def outer(a, za):
+            def inner(b, yb):
+                for n in range(SIDE):
+                    there = wrap(za + n) * (SIDE * SIDE) + wrap(yb + n) * SIDE + across[n]
+                    if n == 0:
+
+                        @pl.when(a + b > 0)
+                        def _():
+                            do(a * (SIDE * SIDE) + b * SIDE, there)
+                    else:
+                        do(a * (SIDE * SIDE) + b * SIDE + n, there)
+                return wrap(yb + 1)
+
+            lax.fori_loop(0, SIDE, inner, y)
+            return wrap(za + 1)
+
+        lax.fori_loop(0, SIDE, outer, z)
 
     def local(src, dst, sem):
         return pltpu.make_async_copy(src, dst, sem)
@@ -65,11 +95,10 @@
     barrier = pltpu.get_barrier_semaphore()
     pl.semaphore_signal(barrier, inc=1, device_id=sibling, device_id_type=MESH)
 
-    def greet(i, c):
-        pl.semaphore_signal(barrier, inc=1, device_id=(chip_at(i), core), device_id_type=MESH)
-        return c
-
-    lax.fori_loop(1, CHIPS, greet, 0)
+    def greet(i, there):
+        pl.semaphore_signal(barrier, inc=1, device_id=(there, core), device_id_type=MESH)
+
+    each_chip(greet)
 
     ins = [
         local(rg, rgb, in_sem.at[0]),
@@ -79,10 +108,9 @@
         local(q.at[:, cols(core, HALF)], qb.at[rows_of(core), :], in_sem.at[4]),
         local(k.at[:, cols(core, KV_HALF)], kb.at[rows_of(core), :], in_sem.at[5]),
         local(v.at[:, cols(core, KV_HALF)], vb.at[rows_of(core), :], in_sem.at[6]),
-        local(ag, gains.at[0], in_sem.at[7]),
-        local(pg, gains.at[1], in_sem.at[8]),
-        local(og, gains.at[2], in_sem.at[9]),
-        local(res, rb, in_sem.at[10]),
+        local(ag, ag_row, in_sem.at[7]),
+        local(pg, pg_row, in_sem.at[8]),
+        local(res, rb, in_sem.at[9]),
     ]
     for c in ins:
         c.start()
@@ -135,14 +163,11 @@
         here = local(packets.at[chip], landing.at[core, 0], recv.at[0])
         here.start()
 
-        def one(i, c):
-            there = chip_at(i)
-            remote(
-                packets.at[there], landing.at[core, i], send, recv.at[lax.div(i, PER_GROUP)], (there, core)
-            ).start()
-            return c
-
-        lax.fori_loop(1, CHIPS, one, 0)
+        def one(i, there):
+            group_of = i // PER_GROUP if isinstance(i, int) else lax.shift_right_logical(i, 3)
+            remote(packets.at[there], landing.at[core, i], send, recv.at[group_of], (there, core)).start()
+
+        each_chip(one)
 
     def scattered(packets, landing, send, recv):
         remote(
@@ -215,26 +240,17 @@
     w_load(gw, 4, SLOTS).start()
     w_load(uw, 4, SLOTS + 1).start()
 
-    def lanes_sum(value):
-        total = value[:, 0:128]
-        for i in range(1, CHUNK // 128):
-            total = total + value[:, i * 128 : (i + 1) * 128]
-        return total
-
-    def sum_halves(landing, send, recv):
-        def one(j, squares):
-            halves(landing, j, send, recv).wait_recv()
-            both = part[rows_of(core), cols(j)].astype(F32) + landing[:, cols(j)].astype(F32)
-            pf[:, cols(j)] = both
-            return squares + lanes_sum(both * both)
-
-        squares = lax.fori_loop(0, CHUNKS, one, jnp.zeros((ROWS, 128), F32))
-        return lax.rsqrt(jnp.sum(squares, axis=-1, keepdims=True) * (1.0 / WIDTH) + EPS)
-
-    scale = sum_halves(prec, pr_send, pr_recv)
+    def sum_halves(j, squares):
+        halves(prec, j, pr_send, pr_recv).wait_recv()
+        both = part[rows_of(core), cols(j)].astype(F32) + prec[:, cols(j)].astype(F32)
+        pf[:, cols(j)] = both
+        return squares + lanes_sum(both * both)
+
+    squares = lax.fori_loop(0, CHUNKS, sum_halves, jnp.zeros((ROWS, 128), F32))
+    scale = lax.rsqrt(jnp.sum(squares, axis=-1, keepdims=True) * (1.0 / WIDTH) + EPS)
 
     def to_packets(j, c):
-        stream = (rb[:, cols(j)].astype(F32) + pf[:, cols(j)] * scale * gains[0, :, cols(j)]).astype(BF)
+        stream = (rb[:, cols(j)].astype(F32) + pf[:, cols(j)] * scale * ag_row[cols(j)].reshape(1, CHUNK)).astype(BF)
         y_rows = jnp.dot(pick, stream, preferred_element_type=F32).astype(BF)
         pks[:, :, cols(j)] = y_rows.reshape(CHIPS, 2, CHUNK)
         return c
@@ -251,14 +267,10 @@
         got = jnp.dot(
             own_place, kvr[:, :, :, cols(j)].reshape(two, CHUNK), preferred_element_type=F32
         ).astype(BF)
-        kvo[2 * j] = got[:, 0:HEAD]
-        kvo[2 * j + 1] = got[:, HEAD:]
-    outs = [
-        local(kvo.at[pl.ds(0, 4)], kc, out_sem.at[0]),
-        local(kvo.at[pl.ds(4, 4)], vc, out_sem.at[1]),
-    ]
-    for c in outs:
-        c.start()
+        kvb[2 * j] = got[:, 0:HEAD]
+        kvb[2 * j + 1] = got[:, HEAD:]
+    outs = [local(kvb, kvo, out_sem.at[0])]
+    outs[0].start()
 
     hand_on(strr, st_recv, stf_send, stf_recv)
 
@@ -273,10 +285,12 @@
     scale = lax.rsqrt(jnp.sum(squares, axis=-1, keepdims=True) * (1.0 / WIDTH) + EPS)
 
     def norm(j, c):
-        xb[:, cols(j)] = (pb[:, cols(j)].astype(F32) * scale * gains[1, :, cols(j)]).astype(BF)
+        xb[:, cols(j)] = (pb[:, cols(j)].astype(F32) * scale * pg_row[cols(j)].reshape(1, CHUNK)).astype(BF)
         return c
 
     lax.fori_loop(0, CHUNKS, norm, 0)
+    outs.append(local(pb.at[rows_of(core), :], own_rows, out_sem.at[1]))
+    outs[1].start()
 
     def weight(unit, i):
         slot = lax.rem(unit, SLOTS)
@@ -321,26 +335,19 @@
 
     lax.fori_loop(0, CHUNKS, projected, 0)
 
+    def kept(j):
+        return local(part.at[rows_of(core), cols(j)], mine.at[:, cols(j)], keep_sem.at[j])
+
     def down(j, c):
         loaded(16 + j)
         for i in range(CHUNK // 256):
             got = jnp.dot(act[...], weight(16 + j, i), preferred_element_type=F32)
             part[:, pl.ds(pl.multiple_of(j * CHUNK + i * 256, 256), 256)] = got.astype(BF)
-        halves(drec, j, dn_send, dn_recv).start()
+        halves(theirs, j, dn_send, dn_recv).start()
+        kept(j).start()
         return c
 
     lax.fori_loop(0, CHUNKS, down, 0)
-    scale = sum_halves(drec, dn_send, dn_recv)
-
-    def finish(j, c):
-        rb[:, cols(j)] = (
-            pb[rows_of(core), cols(j)].astype(F32) + pf[:, cols(j)] * scale * gains[2, :, cols(j)]
-        ).astype(BF)
-        return c
-
-    lax.fori_loop(0, CHUNKS, finish, 0)
-    last_out = local(rb, lo, out_sem.at[2])
-    last_out.start()
 
     for c in exchange:
         c.wait_send()
@@ -355,13 +362,68 @@
     lax.fori_loop(0, GROUPS, sent, 0)
 
     def down_sent(j, c):
-        halves(drec, j, dn_send, dn_recv).wait_send()
+        halves(theirs, j, dn_send, dn_recv).wait()
+        kept(j).wait()
         return c
 
     lax.fori_loop(0, CHUNKS, down_sent, 0)
     for c in outs:
         c.wait()
-    last_out.wait()
+
+
+def last(mine, theirs, own_rows, kvo, og, lo, kc, vc, mb, tb, ob, kvb, og_row, in_sem, kv_sem, og_sem, out_sem):
+    def copy(src, dst, sem):
+        return pltpu.make_async_copy(src, dst, sem)
+
+    pairs = ((mine, mb), (theirs, tb), (own_rows, ob))
+
+    def load(n, j):
+        src, dst = pairs[n]
+        return copy(src.at[:, cols(j)], dst.at[:, cols(j)], in_sem.at[n, j])
+
+    for j in range(CHUNKS):
+        load(0, j).start()
+        load(1, j).start()
+    gain = copy(og, og_row, og_sem)
+    gain.start()
+    for j in range(CHUNKS):
+        load(2, j).start()
+    caches = [
+        copy(kvo.at[pl.ds(0, 4)], kvb.at[pl.ds(0, 4)], kv_sem.at[0]),
+        copy(kvo.at[pl.ds(4, 4)], kvb.at[pl.ds(4, 4)], kv_sem.at[1]),
+    ]
+    for c in caches:
+        c.start()
+    squares = jnp.zeros((ROWS, 128), F32)
+    for j in range(CHUNKS):
+        load(0, j).wait()
+        load(1, j).wait()
+        both = mb[:, cols(j)].astype(F32) + tb[:, cols(j)].astype(F32)
+        squares = squares + lanes_sum(both * both)
+    for c in caches:
+        c.wait()
+    caches = [
+        copy(kvb.at[pl.ds(0, 4)], kc, kv_sem.at[0]),
+        copy(kvb.at[pl.ds(4, 4)], vc, kv_sem.at[1]),
+    ]
+    for c in caches:
+        c.start()
+    scale = lax.rsqrt(jnp.sum(squares, axis=-1, keepdims=True) * (1.0 / WIDTH) + EPS)
+    gain.wait()
+
+    def store(j):
+        return copy(mb.at[:, cols(j)], lo.at[:, cols(j)], out_sem.at[j])
+
+    for j in range(CHUNKS):
+        load(2, j).wait()
+        both = mb[:, cols(j)].astype(F32) + tb[:, cols(j)].astype(F32)
+        row = og_row[cols(j)].reshape(1, CHUNK)
+        mb[:, cols(j)] = (ob[:, cols(j)].astype(F32) + both * scale * row).astype(BF)
+        store(j).start()
+    for j in range(CHUNKS):
+        store(j).wait()
+    for c in caches:
+        c.wait()
 
 
 def per_device(
@@ -381,15 +443,16 @@
 ):
     dma = pltpu.SemaphoreType.DMA
     vmem = pltpu.VMEM
-    return pl.pallas_call(
+    mine, theirs, own_rows, kvo = pl.pallas_call(
         kernel,
         out_shape=(
             jax.ShapeDtypeStruct((ROWS, WIDTH), BF),
-            jax.ShapeDtypeStruct((4, ROWS, HEAD), BF),
-            jax.ShapeDtypeStruct((4, ROWS, HEAD), BF),
-        ),
-        in_specs=[pl.BlockSpec(memory_space=pl.ANY)] * 13,
-        out_specs=(pl.BlockSpec(memory_space=pl.ANY),) * 3,
+            jax.ShapeDtypeStruct((ROWS, WIDTH), BF),
+            jax.ShapeDtypeStruct((ROWS, WIDTH), BF),
+            jax.ShapeDtypeStruct((8, ROWS, HEAD), BF),
+        ),
+        in_specs=[pl.BlockSpec(memory_space=pl.ANY)] * 12,
+        out_specs=(pl.BlockSpec(memory_space=pl.ANY),) * 4,
         scratch_shapes=[
             vmem((SLOTS * WIDTH, CHUNK), BF),
             vmem((2 * ROWS, HALF), BF),
@@ -398,7 +461,8 @@
             vmem((2, 1, ROWS), jnp.int32),
             vmem((ROWS, KV_WIDTH), BF),
             vmem((1, ROWS), jnp.int32),
-            vmem((3, 1, WIDTH), F32),
+            vmem((WIDTH,), F32),
+            vmem((WIDTH,), F32),
             vmem((ROWS, WIDTH), BF),
             vmem((2 * ROWS, HALF), BF),
             vmem((2 * ROWS, WIDTH), BF),
@@ -410,13 +474,13 @@
             vmem((2 * ROWS, WIDTH), BF),
             vmem((2 * ROWS, WIDTH), BF),
             vmem((2 * ROWS, WIDTH), BF),
-            vmem((ROWS, WIDTH), BF),
             vmem((8, ROWS, HEAD), BF),
             vmem((ROWS, WIDTH), F32),
-            dma((11,)),
+            dma((10,)),
             dma((CHUNKS,)),
             dma((SLOTS,)),
-            dma((3,)),
+            dma((2,)),
+            dma((CHUNKS,)),
             dma((4,)),
             dma((4,)),
             dma((CHUNKS,)),
@@ -444,13 +508,35 @@
         segment_ids.reshape(1, ROWS),
         regroup.reshape(1, ROWS),
         out_weight,
-        attn_gain.reshape(1, WIDTH),
-        pre_gain.reshape(1, WIDTH),
+        attn_gain,
+        pre_gain,
         gate_weight,
         up_weight,
         down_weight,
-        post_gain.reshape(1, WIDTH),
     )
+    return pl.pallas_call(
+        last,
+        out_shape=(
+            jax.ShapeDtypeStruct((ROWS, WIDTH), BF),
+            jax.ShapeDtypeStruct((4, ROWS, HEAD), BF),
+            jax.ShapeDtypeStruct((4, ROWS, HEAD), BF),
+        ),
+        in_specs=[pl.BlockSpec(memory_space=pl.ANY)] * 5,
+        out_specs=(pl.BlockSpec(memory_space=pl.ANY),) * 3,
+        scratch_shapes=[
+            vmem((ROWS, WIDTH), BF),
+            vmem((ROWS, WIDTH), BF),
+            vmem((ROWS, WIDTH), BF),
+            vmem((8, ROWS, HEAD), BF),
+            vmem((WIDTH,), F32),
+            dma((3, CHUNKS)),
+            dma((2,)),
+            dma,
+            dma((CHUNKS,)),
+        ],
+        compiler_params=pltpu.CompilerParams(vmem_limit_bytes=62 * 1024 * 1024),
+        name="last",
+    )(mine, theirs, own_rows, kvo, post_gain)
 
 
 def solution(mesh):

time: 74 us -> 64.3 us (0.87)
  local copies, waits for them, and re-layouts: 9.48 us -> 0 us
    unnamed x3 -> x0, local copies, waits for them, and re-layouts: 5.5 us -> none
    reshape x3 -> x0, local copies, waits for them, and re-layouts: 3.98 us -> none  [the longest x1 1.33 us: per_device(): attn_gain.reshape(1, WIDTH)]
    pallas_call x0 -> x1, Pallas kernels: none -> 3.5 us  [per_device(): pl.pallas_call(last, out_shape=(jax.ShapeDtypeStruct((ROWS, WIDTH), BF),...]
    pallas_call x1, Pallas kernels: 63.5 us -> 60.1 us  [per_device(): pl.pallas_call(kernel, out_shape=(jax.ShapeDtypeStruct((ROWS, WIDTH), BF)...]
where the time goes in v2:
time: 64.3 us; the launch traced here: 64.2 us
  Pallas kernels  63.6 us (99%)
    pallas_call x1, Pallas kernels, per_device(): pl.pallas_call(kernel, out_shape=(jax.ShapeDtypeStruct((ROWS, WIDTH), BF)...  60.1 us
    pallas_call x1, Pallas kernels, per_device(): pl.pallas_call(last, out_shape=(jax.ShapeDtypeStruct((ROWS, WIDTH), BF),...  3.5 us

profile of v2, /device:TPU:1, one launch (start us, length us, event | category | flops | bytes accessed | tf_op | source)
XLA Modules:
  0.0 64.2 jit_solution(13415642366606783881)
XLA Ops:
  0.6 60.1 %layer.1 = (bf16[128,3584]{1,0:T(8,128)(2,1)}, bf16[128,3584]{1,0:T(8,128)(2,1)}, bf16[128,3584]{1,0:T(8,128)(2,1)}, bf16[8,128,256]{2,1,0:T(8,128)(2,1)}) custom-call(bf16[128,2048]{1,0:T(8,128)(2,1)} %q.1, bf16[128,1024]{1,0:T(8,128)(2,1)} %k.1, bf16[128,1024]{1,0:T(8,128)(2,1)} %v.1, bf16[128,3584]{1,0:T(8,128)(2,1)} %res.1, s32[1,128]{1,0:T(1,128)} %bitcast.2, ...), custom_call_target="tpu_custom_call" | custom-call | tf_op jit(solution)/shard_map/layer/pallas_call | solution.py:446
  60.7 3.5 %last.1 = (bf16[128,3584]{1,0:T(8,128)(2,1)}, bf16[4,128,256]{2,1,0:T(8,128)(2,1)}, bf16[4,128,256]{2,1,0:T(8,128)(2,1)}) custom-call(bf16[128,3584]{1,0:T(8,128)(2,1)} %get-tuple-element.7.mine, bf16[128,3584]{1,0:T(8,128)(2,1)} %get-tuple-element.8.theirs, bf16[128,3584]{1,0:T(8,128)(2,1)} %get-tuple-element.9.own_rows, ...), custom_call_target="tpu_custom_call" | custom-call | tf_op jit(solution)/shard_map/last/pallas_call | solution.py:517

commit v3 on v2

--- a/solution.py
+++ b/solution.py
@@ -17,7 +17,13 @@
 KV_WIDTH = 2048
 CHUNK = 512
 CHUNKS = WIDTH // CHUNK
-SLOTS = 10
+FIRST = 3
+SECOND = CHUNKS - FIRST
+A_ROWS = FIRST * CHUNK
+B_ROWS = SECOND * CHUNK
+UNITS = 2 * CHUNKS
+B_SLOTS = 8
+B_BASE = UNITS * A_ROWS
 GROUPS = 8
 PER_GROUP = CHIPS // GROUPS
 CAP = 50.0
@@ -46,10 +52,11 @@
 def kernel(
     q, k, v, res, seg, rg, ow, ag, pg, gw, uw, dw,
     mine, theirs, own_rows, kvo,
-    wbuf, qb, kb, vb, segb, kvl, rgb, ag_row, pg_row, rb, att, part, prec, pkv, kvr, pks, strr,
-    pb, xb, act, kvb, pf,
-    in_sem, o_sem, w_sem, out_sem, keep_sem, ex_send, ex_recv, pr_send, pr_recv, dn_send, dn_recv,
-    kv_send, kv_recv, kvf_send, kvf_recv, st_send, st_recv, stf_send, stf_recv,
+    wbuf, qb, kb, vb, segb, kvl, rgb, ag_row, pg_row, rb, att, part, prec, pkv, kvr, pka, pkb, sta, stb,
+    xb, act, kvb, gacc, uacc,
+    in_sem, o_sem, a_sem, b_sem, d_sem, out_sem, keep_sem, ex_send, ex_recv, pr_send, pr_recv, dn_send, dn_recv,
+    kv_send, kv_recv, kvf_send, kvf_recv,
+    sa_send, sa_recv, saf_send, saf_recv, sb_send, sb_recv, sbf_send, sbf_recv,
 ):
     chip = lax.axis_index("req")
     core = lax.axis_index("kv")
@@ -115,19 +122,29 @@
     for c in ins:
         c.start()
 
+    def wrows(start, count):
+        return wbuf.at[pl.ds(pl.multiple_of(start, CHUNK), count), :]
+
     def o_load(j):
-        return local(ow.at[:, cols(j)], wbuf.at[pl.ds(pl.multiple_of(j * HALF, HALF), HALF), :], o_sem.at[j])
+        return local(ow.at[:, cols(j)], wrows(B_BASE + j * HALF, HALF), o_sem.at[j])
 
     for j in range(CHUNKS):
         o_load(j).start()
 
-    def w_load(src, j, unit):
-        slot = lax.rem(unit, SLOTS) if not isinstance(unit, int) else unit % SLOTS
-        return local(
-            src.at[:, cols(j)],
-            wbuf.at[pl.ds(pl.multiple_of(slot * WIDTH, WIDTH), WIDTH), :],
-            w_sem.at[slot],
-        )
+    def a_load(src, j, unit):
+        return local(src.at[pl.ds(0, A_ROWS), cols(j)], wrows(unit * A_ROWS, A_ROWS), a_sem.at[unit])
+
+    def b_start(unit):
+        return B_BASE + lax.rem(unit, B_SLOTS) * B_ROWS
+
+    def b_load(src, j, unit):
+        return local(src.at[pl.ds(A_ROWS, B_ROWS), cols(j)], wrows(b_start(unit), B_ROWS), b_sem.at[unit])
+
+    def d_start(j):
+        return jnp.where(j < CHUNKS - 1, j * WIDTH, B_BASE + 6 * B_ROWS)
+
+    def d_load(j):
+        return local(dw.at[:, cols(j)], wrows(d_start(j), WIDTH), d_sem.at[j])
 
     for c in ins[:3]:
         c.wait()
@@ -182,26 +199,33 @@
             landing.at[core, group(i)], landing.at[core, group(i)], send.at[i], recv.at[i], sibling
         )
 
-    def hand_on(landing, recv, send_f, recv_f):
+    def hand_on(landing, i, recv, send_f, recv_f):
+        block = landing.at[core, group(i)]
+        local(block, block, recv.at[i]).wait()
+        forward(landing, i, send_f, recv_f).start()
+
+    def arrive(landing, send_f, recv_f):
         def one(i, c):
-            block = landing.at[core, group(i)]
-            local(block, block, recv.at[i]).wait()
-            forward(landing, i, send_f, recv_f).start()
-            return c
-
-        lax.fori_loop(0, GROUPS, one, 0)
-
-        def arrived(i, c):
             theirs = landing.at[other, group(i)]
             remote(theirs, theirs, send_f.at[i], recv_f.at[i], sibling).wait_recv()
             return c
 
-        lax.fori_loop(0, GROUPS, arrived, 0)
+        lax.fori_loop(0, GROUPS, one, 0)
+
+    def hand_on_all(landing, recv, send_f, recv_f):
+        def one(i, c):
+            hand_on(landing, i, recv, send_f, recv_f)
+            return c
+
+        lax.fori_loop(0, GROUPS, one, 0)
+        arrive(landing, send_f, recv_f)
 
     scatter(pkv, kvr, kv_send, kv_recv)
 
-    for unit in range(2, SLOTS):
-        w_load(gw if unit % 2 == 0 else uw, (unit - 2) // 2, unit).start()
+    for unit in range(UNITS):
+        a_load((gw, uw)[unit % 2], unit // 2, unit).start()
+    for unit in range(4, B_SLOTS):
+        b_load((gw, uw)[unit % 2], unit // 2, unit).start()
 
     for c in ins[3:]:
         c.wait()
@@ -231,34 +255,41 @@
 
     def project(j, c):
         o_load(j).wait()
-        w = wbuf[pl.ds(pl.multiple_of(j * HALF, HALF), HALF), :]
+        w = wrows(B_BASE + j * HALF, HALF)[...]
         part[:, cols(j)] = jnp.dot(att[...], w, preferred_element_type=F32).astype(BF)
         halves(prec, j, pr_send, pr_recv).start()
         return c
 
     lax.fori_loop(0, CHUNKS, project, 0)
-    w_load(gw, 4, SLOTS).start()
-    w_load(uw, 4, SLOTS + 1).start()
+    for unit in range(4):
+        b_load((gw, uw)[unit % 2], unit // 2, unit).start()
 
     def sum_halves(j, squares):
         halves(prec, j, pr_send, pr_recv).wait_recv()
         both = part[rows_of(core), cols(j)].astype(F32) + prec[:, cols(j)].astype(F32)
-        pf[:, cols(j)] = both
+        gacc[0:ROWS, cols(j)] = both
         return squares + lanes_sum(both * both)
 
     squares = lax.fori_loop(0, CHUNKS, sum_halves, jnp.zeros((ROWS, 128), F32))
     scale = lax.rsqrt(jnp.sum(squares, axis=-1, keepdims=True) * (1.0 / WIDTH) + EPS)
 
-    def to_packets(j, c):
-        stream = (rb[:, cols(j)].astype(F32) + pf[:, cols(j)] * scale * ag_row[cols(j)].reshape(1, CHUNK)).astype(BF)
-        y_rows = jnp.dot(pick, stream, preferred_element_type=F32).astype(BF)
-        pks[:, :, cols(j)] = y_rows.reshape(CHIPS, 2, CHUNK)
-        return c
-
-    lax.fori_loop(0, CHUNKS, to_packets, 0)
-    scatter(pks, strr, st_send, st_recv)
-
-    hand_on(kvr, kv_recv, kvf_send, kvf_recv)
+    def to_packets(packets, first):
+        def one(j, c):
+            at = cols(first + j)
+            added = gacc[0:ROWS, at] * scale * ag_row[at].reshape(1, CHUNK)
+            stream = (rb[:, at].astype(F32) + added).astype(BF)
+            y_rows = jnp.dot(pick, stream, preferred_element_type=F32).astype(BF)
+            packets[:, :, cols(j)] = y_rows.reshape(CHIPS, 2, CHUNK)
+            return c
+
+        return one
+
+    lax.fori_loop(0, FIRST, to_packets(pka, 0), 0)
+    scatter(pka, sta, sa_send, sa_recv)
+    lax.fori_loop(0, SECOND, to_packets(pkb, FIRST), 0)
+    scatter(pkb, stb, sb_send, sb_recv)
+
+    hand_on_all(kvr, kv_recv, kvf_send, kvf_recv)
     at = kvr[:, :, :, KV_WIDTH:].reshape(two, 128).astype(F32)
     at = jnp.transpose(at)[0:1, :].astype(jnp.int32)
     place = (t_at == at).astype(BF)
@@ -272,58 +303,67 @@
     outs = [local(kvb, kvo, out_sem.at[0])]
     outs[0].start()
 
-    hand_on(strr, st_recv, stf_send, stf_recv)
-
-    def put(j, squares):
-        got = jnp.dot(
-            place, strr[:, :, :, cols(j)].reshape(two, CHUNK), preferred_element_type=F32
-        )
-        pb[:, cols(j)] = got.astype(BF)
-        return squares + lanes_sum(got * got)
-
-    squares = lax.fori_loop(0, CHUNKS, put, jnp.zeros((two, 128), F32))
+    def put(landing, first):
+        def one(j, squares):
+            rows = landing[:, :, :, cols(j)].reshape(two, CHUNK)
+            got = jnp.dot(place, rows, preferred_element_type=F32)
+            at = cols(first + j)
+            xb[:, at] = (got * pg_row[at].reshape(1, CHUNK)).astype(BF)
+            rb[:, at] = jnp.dot(own_place, rows, preferred_element_type=F32).astype(BF)
+            return squares + lanes_sum(got * got)
+
+        return one
+
+    hand_on_all(sta, sa_recv, saf_send, saf_recv)
+    squares = lax.fori_loop(0, FIRST, put(sta, 0), jnp.zeros((two, 128), F32))
+
+    def product(first, depth, start, i):
+        w = wbuf[pl.ds(pl.multiple_of(start, CHUNK), depth), pl.ds(i * 256, 256)]
+        return jnp.dot(xb[:, pl.ds(first, depth)], w, preferred_element_type=F32)
+
+    def at256(j, i):
+        return pl.ds(pl.multiple_of(j * CHUNK + i * 256, 256), 256)
+
+    def begin(j, c):
+        for m in range(2):
+            a_load(gw, j, 2 * j + m).wait()
+        for i in range(CHUNK // 256):
+            gacc[:, at256(j, i)] = product(0, A_ROWS, 2 * j * A_ROWS, i)
+            uacc[:, at256(j, i)] = product(0, A_ROWS, (2 * j + 1) * A_ROWS, i)
+
+        @pl.when(j > 0)
+        def _():
+            d_load(j - 1).start()
+
+        hand_on(stb, j, sb_recv, sbf_send, sbf_recv)
+        return c
+
+    lax.fori_loop(0, CHUNKS, begin, 0)
+    hand_on(stb, CHUNKS, sb_recv, sbf_send, sbf_recv)
+    arrive(stb, sbf_send, sbf_recv)
+    squares = lax.fori_loop(0, SECOND, put(stb, FIRST), squares)
     scale = lax.rsqrt(jnp.sum(squares, axis=-1, keepdims=True) * (1.0 / WIDTH) + EPS)
-
-    def norm(j, c):
-        xb[:, cols(j)] = (pb[:, cols(j)].astype(F32) * scale * pg_row[cols(j)].reshape(1, CHUNK)).astype(BF)
-        return c
-
-    lax.fori_loop(0, CHUNKS, norm, 0)
-    outs.append(local(pb.at[rows_of(core), :], own_rows, out_sem.at[1]))
+    outs.append(local(rb, own_rows, out_sem.at[1]))
     outs[1].start()
 
-    def weight(unit, i):
-        slot = lax.rem(unit, SLOTS)
-        return wbuf[
-            pl.ds(pl.multiple_of(slot * WIDTH, WIDTH), WIDTH), pl.ds(i * 256, 256)
-        ]
-
-    def loaded(unit):
-        slot = lax.rem(unit, SLOTS)
-        block = wbuf.at[pl.ds(pl.multiple_of(slot * WIDTH, WIDTH), WIDTH), :]
-        local(block, block, w_sem.at[slot]).wait()
-
     def hidden(j, c):
-        loaded(2 + 2 * j)
-        loaded(3 + 2 * j)
+        for m in range(2):
+            b_load(gw, j, 2 * j + m).wait()
         for i in range(CHUNK // 256):
-            u = jnp.dot(xb[...], weight(2 + 2 * j, i), preferred_element_type=F32)
-            up = jnp.dot(xb[...], weight(3 + 2 * j, i), preferred_element_type=F32)
+            at = at256(j, i)
+            u = (gacc[:, at] + product(A_ROWS, B_ROWS, b_start(2 * j), i)) * scale
+            up = (uacc[:, at] + product(A_ROWS, B_ROWS, b_start(2 * j + 1), i)) * scale
             gelu = 0.5 * u * (1.0 + jnp.tanh(0.7978845608028654 * (u + 0.044715 * (u * u * u))))
-            act[:, pl.ds(pl.multiple_of(j * CHUNK + i * 256, 256), 256)] = (gelu * up).astype(BF)
-
-        @pl.when(j < 2)
+            act[:, at] = (gelu * up).astype(BF)
+
+        @pl.when(j < CHUNKS - B_SLOTS // 2)
         def _():
-            w_load(gw, 5 + j, 12 + 2 * j).start()
-            w_load(uw, 5 + j, 13 + 2 * j).start()
-
-        @pl.when((j >= 2) & (j < 6))
+            b_load(gw, j + B_SLOTS // 2, 2 * j + B_SLOTS).start()
+            b_load(uw, j + B_SLOTS // 2, 2 * j + 1 + B_SLOTS).start()
+
+        @pl.when(j == CHUNKS - B_SLOTS // 2)
         def _():
-            w_load(dw, 2 * (j - 2), 12 + 2 * j).start()
-
-        @pl.when((j >= 2) & (j < 5))
-        def _():
-            w_load(dw, 2 * (j - 2) + 1, 13 + 2 * j).start()
+            d_load(CHUNKS - 1).start()
 
         return c
 
@@ -339,10 +379,10 @@
         return local(part.at[rows_of(core), cols(j)], mine.at[:, cols(j)], keep_sem.at[j])
 
     def down(j, c):
-        loaded(16 + j)
+        d_load(j).wait()
         for i in range(CHUNK // 256):
-            got = jnp.dot(act[...], weight(16 + j, i), preferred_element_type=F32)
-            part[:, pl.ds(pl.multiple_of(j * CHUNK + i * 256, 256), 256)] = got.astype(BF)
+            w = wbuf[pl.ds(pl.multiple_of(d_start(j), CHUNK), WIDTH), pl.ds(i * 256, 256)]
+            part[:, at256(j, i)] = jnp.dot(act[...], w, preferred_element_type=F32).astype(BF)
         halves(theirs, j, dn_send, dn_recv).start()
         kept(j).start()
         return c
@@ -352,11 +392,13 @@
     for c in exchange:
         c.wait_send()
     scattered(pkv, kvr, kv_send, kv_recv)
-    scattered(pks, strr, st_send, st_recv)
+    scattered(pka, sta, sa_send, sa_recv)
+    scattered(pkb, stb, sb_send, sb_recv)
 
     def sent(i, c):
         forward(kvr, i, kvf_send, kvf_recv).wait_send()
-        forward(strr, i, stf_send, stf_recv).wait_send()
+        forward(sta, i, saf_send, saf_recv).wait_send()
+        forward(stb, i, sbf_send, sbf_recv).wait_send()
         return c
 
     lax.fori_loop(0, GROUPS, sent, 0)
@@ -454,7 +496,7 @@
         in_specs=[pl.BlockSpec(memory_space=pl.ANY)] * 12,
         out_specs=(pl.BlockSpec(memory_space=pl.ANY),) * 4,
         scratch_shapes=[
-            vmem((SLOTS * WIDTH, CHUNK), BF),
+            vmem((B_BASE + B_SLOTS * B_ROWS, CHUNK), BF),
             vmem((2 * ROWS, HALF), BF),
             vmem((2 * ROWS, KV_HALF), BF),
             vmem((2 * ROWS, KV_HALF), BF),
@@ -469,16 +511,20 @@
             vmem((ROWS, WIDTH), BF),
             vmem((CHIPS, 2, KV_WIDTH + 128), BF),
             vmem((2, CHIPS, 2, KV_WIDTH + 128), BF),
-            vmem((CHIPS, 2, WIDTH), BF),
-            vmem((2, CHIPS, 2, WIDTH), BF),
-            vmem((2 * ROWS, WIDTH), BF),
+            vmem((CHIPS, 2, A_ROWS), BF),
+            vmem((CHIPS, 2, B_ROWS), BF),
+            vmem((2, CHIPS, 2, A_ROWS), BF),
+            vmem((2, CHIPS, 2, B_ROWS), BF),
             vmem((2 * ROWS, WIDTH), BF),
             vmem((2 * ROWS, WIDTH), BF),
             vmem((8, ROWS, HEAD), BF),
-            vmem((ROWS, WIDTH), F32),
+            vmem((2 * ROWS, WIDTH), F32),
+            vmem((2 * ROWS, WIDTH), F32),
             dma((10,)),
             dma((CHUNKS,)),
-            dma((SLOTS,)),
+            dma((UNITS,)),
+            dma((UNITS,)),
+            dma((CHUNKS,)),
             dma((2,)),
             dma((CHUNKS,)),
             dma((4,)),
@@ -487,14 +533,7 @@
             dma((CHUNKS,)),
             dma((CHUNKS,)),
             dma((CHUNKS,)),
-            dma,
-            dma((GROUPS,)),
-            dma((GROUPS,)),
-            dma((GROUPS,)),
-            dma,
-            dma((GROUPS,)),
-            dma((GROUPS,)),
-            dma((GROUPS,)),
+            *[dma, dma((GROUPS,)), dma((GROUPS,)), dma((GROUPS,))] * 3,
         ],
         compiler_params=pltpu.CompilerParams(
             collective_id=0, has_side_effects=True, vmem_limit_bytes=62 * 1024 * 1024

time: 64.3 us -> 62.2 us (0.967)
  Pallas kernels: 63.6 us -> 61.5 us
    pallas_call x1, Pallas kernels: 60.1 us -> 58 us  [per_device(): pl.pallas_call(kernel, out_shape=(jax.ShapeDtypeStruct((ROWS, WIDTH), BF)...]
where the time goes in v3:
time: 62.2 us; the launch traced here: 62.1 us
  Pallas kernels  61.5 us (99%)
  between operations  0.64 us (1%)
    pallas_call x1, Pallas kernels, per_device(): pl.pallas_call(kernel, out_shape=(jax.ShapeDtypeStruct((ROWS, WIDTH), BF)...  58 us
    pallas_call x1, Pallas kernels, per_device(): pl.pallas_call(last, out_shape=(jax.ShapeDtypeStruct((ROWS, WIDTH), BF),...  3.5 us

profile of v3, /device:TPU:1, one launch (start us, length us, event | category | flops | bytes accessed | tf_op | source)
XLA Modules:
  0.0 62.1 jit_solution(7249083708960032866)
XLA Ops:
  0.6 58.0 %layer.1 = (bf16[128,3584]{1,0:T(8,128)(2,1)}, bf16[128,3584]{1,0:T(8,128)(2,1)}, bf16[128,3584]{1,0:T(8,128)(2,1)}, bf16[8,128,256]{2,1,0:T(8,128)(2,1)}) custom-call(bf16[128,2048]{1,0:T(8,128)(2,1)} %q.1, bf16[128,1024]{1,0:T(8,128)(2,1)} %k.1, bf16[128,1024]{1,0:T(8,128)(2,1)} %v.1, bf16[128,3584]{1,0:T(8,128)(2,1)} %res.1, s32[1,128]{1,0:T(1,128)} %bitcast.2, ...), custom_call_target="tpu_custom_call" | custom-call | tf_op jit(solution)/shard_map/layer/pallas_call | solution.py:488
  58.6 3.5 %last.1 = (bf16[128,3584]{1,0:T(8,128)(2,1)}, bf16[4,128,256]{2,1,0:T(8,128)(2,1)}, bf16[4,128,256]{2,1,0:T(8,128)(2,1)}) custom-call(bf16[128,3584]{1,0:T(8,128)(2,1)} %get-tuple-element.7.mine, bf16[128,3584]{1,0:T(8,128)(2,1)} %get-tuple-element.8.theirs, bf16[128,3584]{1,0:T(8,128)(2,1)} %get-tuple-element.9.own_rows, ...), custom_call_target="tpu_custom_call" | custom-call | tf_op jit(solution)/shard_map/last/pallas_call | solution.py:556

commit v4 on v3

--- a/solution.py
+++ b/solution.py
@@ -53,8 +53,8 @@
     q, k, v, res, seg, rg, ow, ag, pg, gw, uw, dw,
     mine, theirs, own_rows, kvo,
     wbuf, qb, kb, vb, segb, kvl, rgb, ag_row, pg_row, rb, att, part, prec, pkv, kvr, pka, pkb, sta, stb,
-    xb, act, kvb, gacc, uacc,
-    in_sem, o_sem, a_sem, b_sem, d_sem, out_sem, keep_sem, ex_send, ex_recv, pr_send, pr_recv, dn_send, dn_recv,
+    xb, act, gacc, uacc,
+    in_sem, o_sem, a_sem, b_sem, d_sem, keep_sem, ex_send, ex_recv, pr_send, pr_recv, dn_send, dn_recv,
     kv_send, kv_recv, kvf_send, kvf_recv,
     sa_send, sa_recv, saf_send, saf_recv, sb_send, sb_recv, sbf_send, sbf_recv,
 ):
@@ -287,7 +287,6 @@
     lax.fori_loop(0, FIRST, to_packets(pka, 0), 0)
     scatter(pka, sta, sa_send, sa_recv)
     lax.fori_loop(0, SECOND, to_packets(pkb, FIRST), 0)
-    scatter(pkb, stb, sb_send, sb_recv)
 
     hand_on_all(kvr, kv_recv, kvf_send, kvf_recv)
     at = kvr[:, :, :, KV_WIDTH:].reshape(two, 128).astype(F32)
@@ -298,10 +297,8 @@
         got = jnp.dot(
             own_place, kvr[:, :, :, cols(j)].reshape(two, CHUNK), preferred_element_type=F32
         ).astype(BF)
-        kvb[2 * j] = got[:, 0:HEAD]
-        kvb[2 * j + 1] = got[:, HEAD:]
-    outs = [local(kvb, kvo, out_sem.at[0])]
-    outs[0].start()
+        kvo[2 * j] = got[:, 0:HEAD]
+        kvo[2 * j + 1] = got[:, HEAD:]
 
     def put(landing, first):
         def one(j, squares):
@@ -309,11 +306,12 @@
             got = jnp.dot(place, rows, preferred_element_type=F32)
             at = cols(first + j)
             xb[:, at] = (got * pg_row[at].reshape(1, CHUNK)).astype(BF)
-            rb[:, at] = jnp.dot(own_place, rows, preferred_element_type=F32).astype(BF)
+            own_rows[:, at] = jnp.dot(own_place, rows, preferred_element_type=F32).astype(BF)
             return squares + lanes_sum(got * got)
 
         return one
 
+    scatter(pkb, stb, sb_send, sb_recv)
     hand_on_all(sta, sa_recv, saf_send, saf_recv)
     squares = lax.fori_loop(0, FIRST, put(sta, 0), jnp.zeros((two, 128), F32))
 
@@ -343,8 +341,6 @@
     arrive(stb, sbf_send, sbf_recv)
     squares = lax.fori_loop(0, SECOND, put(stb, FIRST), squares)
     scale = lax.rsqrt(jnp.sum(squares, axis=-1, keepdims=True) * (1.0 / WIDTH) + EPS)
-    outs.append(local(rb, own_rows, out_sem.at[1]))
-    outs[1].start()
 
     def hidden(j, c):
         for m in range(2):
@@ -409,58 +405,34 @@
         return c
 
     lax.fori_loop(0, CHUNKS, down_sent, 0)
-    for c in outs:
-        c.wait()
-
-
-def last(mine, theirs, own_rows, kvo, og, lo, kc, vc, mb, tb, ob, kvb, og_row, in_sem, kv_sem, og_sem, out_sem):
+
+
+def last(mine, theirs, own_rows, kvo, og, lo, kc, vc, rows, og_row, kv_sem, og_sem, out_sem):
     def copy(src, dst, sem):
         return pltpu.make_async_copy(src, dst, sem)
 
-    pairs = ((mine, mb), (theirs, tb), (own_rows, ob))
-
-    def load(n, j):
-        src, dst = pairs[n]
-        return copy(src.at[:, cols(j)], dst.at[:, cols(j)], in_sem.at[n, j])
-
-    for j in range(CHUNKS):
-        load(0, j).start()
-        load(1, j).start()
     gain = copy(og, og_row, og_sem)
     gain.start()
-    for j in range(CHUNKS):
-        load(2, j).start()
     caches = [
-        copy(kvo.at[pl.ds(0, 4)], kvb.at[pl.ds(0, 4)], kv_sem.at[0]),
-        copy(kvo.at[pl.ds(4, 4)], kvb.at[pl.ds(4, 4)], kv_sem.at[1]),
+        copy(kvo.at[pl.ds(0, 4)], kc, kv_sem.at[0]),
+        copy(kvo.at[pl.ds(4, 4)], vc, kv_sem.at[1]),
     ]
     for c in caches:
         c.start()
     squares = jnp.zeros((ROWS, 128), F32)
     for j in range(CHUNKS):
-        load(0, j).wait()
-        load(1, j).wait()
-        both = mb[:, cols(j)].astype(F32) + tb[:, cols(j)].astype(F32)
+        both = mine[:, cols(j)].astype(F32) + theirs[:, cols(j)].astype(F32)
         squares = squares + lanes_sum(both * both)
-    for c in caches:
-        c.wait()
-    caches = [
-        copy(kvb.at[pl.ds(0, 4)], kc, kv_sem.at[0]),
-        copy(kvb.at[pl.ds(4, 4)], vc, kv_sem.at[1]),
-    ]
-    for c in caches:
-        c.start()
     scale = lax.rsqrt(jnp.sum(squares, axis=-1, keepdims=True) * (1.0 / WIDTH) + EPS)
     gain.wait()
 
     def store(j):
-        return copy(mb.at[:, cols(j)], lo.at[:, cols(j)], out_sem.at[j])
+        return copy(rows.at[:, cols(j)], lo.at[:, cols(j)], out_sem.at[j])
 
     for j in range(CHUNKS):
-        load(2, j).wait()
-        both = mb[:, cols(j)].astype(F32) + tb[:, cols(j)].astype(F32)
+        both = mine[:, cols(j)].astype(F32) + theirs[:, cols(j)].astype(F32)
         row = og_row[cols(j)].reshape(1, CHUNK)
-        mb[:, cols(j)] = (ob[:, cols(j)].astype(F32) + both * scale * row).astype(BF)
+        rows[:, cols(j)] = (own_rows[:, cols(j)].astype(F32) + both * scale * row).astype(BF)
         store(j).start()
     for j in range(CHUNKS):
         store(j).wait()
@@ -488,13 +460,13 @@
     mine, theirs, own_rows, kvo = pl.pallas_call(
         kernel,
         out_shape=(
-            jax.ShapeDtypeStruct((ROWS, WIDTH), BF),
-            jax.ShapeDtypeStruct((ROWS, WIDTH), BF),
-            jax.ShapeDtypeStruct((ROWS, WIDTH), BF),
-            jax.ShapeDtypeStruct((8, ROWS, HEAD), BF),
+            vmem((ROWS, WIDTH), BF),
+            vmem((ROWS, WIDTH), BF),
+            vmem((ROWS, WIDTH), BF),
+            vmem((8, ROWS, HEAD), BF),
         ),
         in_specs=[pl.BlockSpec(memory_space=pl.ANY)] * 12,
-        out_specs=(pl.BlockSpec(memory_space=pl.ANY),) * 4,
+        out_specs=(pl.BlockSpec(memory_space=vmem),) * 4,
         scratch_shapes=[
             vmem((B_BASE + B_SLOTS * B_ROWS, CHUNK), BF),
             vmem((2 * ROWS, HALF), BF),
@@ -517,7 +489,6 @@
             vmem((2, CHIPS, 2, B_ROWS), BF),
             vmem((2 * ROWS, WIDTH), BF),
             vmem((2 * ROWS, WIDTH), BF),
-            vmem((8, ROWS, HEAD), BF),
             vmem((2 * ROWS, WIDTH), F32),
             vmem((2 * ROWS, WIDTH), F32),
             dma((10,)),
@@ -525,7 +496,6 @@
             dma((UNITS,)),
             dma((UNITS,)),
             dma((CHUNKS,)),
-            dma((2,)),
             dma((CHUNKS,)),
             dma((4,)),
             dma((4,)),
@@ -536,7 +506,7 @@
             *[dma, dma((GROUPS,)), dma((GROUPS,)), dma((GROUPS,))] * 3,
         ],
         compiler_params=pltpu.CompilerParams(
-            collective_id=0, has_side_effects=True, vmem_limit_bytes=62 * 1024 * 1024
+            collective_id=0, has_side_effects=True, vmem_limit_bytes=60 * 1024 * 1024
         ),
         name="layer",
     )(
@@ -560,22 +530,18 @@
             jax.ShapeDtypeStruct((4, ROWS, HEAD), BF),
             jax.ShapeDtypeStruct((4, ROWS, HEAD), BF),
         ),
-        in_specs=[pl.BlockSpec(memory_space=pl.ANY)] * 5,
+        in_specs=[pl.BlockSpec(memory_space=vmem)] * 4 + [pl.BlockSpec(memory_space=pl.ANY)],
         out_specs=(pl.BlockSpec(memory_space=pl.ANY),) * 3,
         scratch_shapes=[
             vmem((ROWS, WIDTH), BF),
-            vmem((ROWS, WIDTH), BF),
-            vmem((ROWS, WIDTH), BF),
-            vmem((8, ROWS, HEAD), BF),
             vmem((WIDTH,), F32),
-            dma((3, CHUNKS)),
             dma((2,)),
             dma,
             dma((CHUNKS,)),
         ],
-        compiler_params=pltpu.CompilerParams(vmem_limit_bytes=62 * 1024 * 1024),
+        compiler_params=pltpu.CompilerParams(vmem_limit_bytes=60 * 1024 * 1024),
         name="last",
-    )(mine, theirs, own_rows, kvo, post_gain)
+    )(*(pltpu.with_memory_space_constraint(r, vmem) for r in (mine, theirs, own_rows, kvo)), post_gain)
 
 
 def solution(mesh):

time: 62.2 us -> 59.6 us (0.958)
  Pallas kernels: 61.5 us -> 58.8 us
    pallas_call x1, Pallas kernels: 3.5 us -> 1.91 us  [per_device(): pl.pallas_call(last, out_shape=(jax.ShapeDtypeStruct((ROWS, WIDTH), BF),...]
    pallas_call x1, Pallas kernels: 58 us -> 56.9 us  [per_device(): pl.pallas_call(kernel, out_shape=(vmem((ROWS, WIDTH), BF), vmem((ROWS, WI...]
where the time goes in v4:
time: 59.6 us; the launch traced here: 59.4 us
  Pallas kernels  58.8 us (99%)
  between operations  0.64 us (1%)
    pallas_call x1, Pallas kernels, per_device(): pl.pallas_call(kernel, out_shape=(vmem((ROWS, WIDTH), BF), vmem((ROWS, WI...  56.9 us
    pallas_call x1, Pallas kernels, per_device(): pl.pallas_call(last, out_shape=(jax.ShapeDtypeStruct((ROWS, WIDTH), BF),...  1.91 us

profile of v4, /device:TPU:1, one launch (start us, length us, event | category | flops | bytes accessed | tf_op | source)
XLA Modules:
  0.0 59.4 jit_solution(111570175369041351)
XLA Ops:
  0.6 56.9 %layer.1 = (bf16[128,3584]{1,0:T(8,128)(2,1)S(1)}, bf16[128,3584]{1,0:T(8,128)(2,1)S(1)}, bf16[128,3584]{1,0:T(8,128)(2,1)S(1)}, bf16[8,128,256]{2,1,0:T(8,128)(2,1)S(1)}) custom-call(bf16[128,2048]{1,0:T(8,128)(2,1)} %q.1, bf16[128,1024]{1,0:T(8,128)(2,1)} %k.1, bf16[128,1024]{1,0:T(8,128)(2,1)} %v.1, bf16[128,3584]{1,0:T(8,128)(2,1)} %res.1, ...), custom_call_target="tpu_custom_call" | custom-call | tf_op jit(solution)/shard_map/layer/pallas_call | solution.py:460
  57.5 1.9 %last.1 = (bf16[128,3584]{1,0:T(8,128)(2,1)}, bf16[4,128,256]{2,1,0:T(8,128)(2,1)}, bf16[4,128,256]{2,1,0:T(8,128)(2,1)}) custom-call(bf16[128,3584]{1,0:T(8,128)(2,1)S(1)} %get-tuple-element.7.mine, bf16[128,3584]{1,0:T(8,128)(2,1)S(1)} %get-tuple-element.8.theirs, bf16[128,3584]{1,0:T(8,128)(2,1)S(1)} %get-tuple-element.9.own_rows, ...), custom_call_target="tpu_custom_call" | custom-call | tf_op jit(solution)/shard_map/last/pallas_call | solution.py:526

commit v5 on v4

--- a/solution.py
+++ b/solution.py
@@ -227,9 +227,9 @@
     for unit in range(4, B_SLOTS):
         b_load((gw, uw)[unit % 2], unit // 2, unit).start()
 
-    for c in ins[3:]:
+    for c in ins[3:7]:
         c.wait()
-    for c in exchange:
+    for c in exchange[:3]:
         c.wait_recv()
     two = 2 * ROWS
     t_at = lax.broadcasted_iota(jnp.int32, (two, two), 0)
@@ -245,6 +245,8 @@
         scores = CAP * jnp.tanh(raw * (HEAD**-0.5 / CAP))
         probs = jnp.where(allowed, jnp.exp(scores), 0.0)
         totals = jnp.sum(probs, axis=-1, keepdims=True)
+        if h == 0:
+            exchange[3].wait_recv()
         mixed = jnp.dot(probs.astype(BF), vb[:, key], preferred_element_type=F32)
         att[:, own] = (mixed * (1.0 / totals)).astype(BF)
 
@@ -284,6 +286,8 @@
 
         return one
 
+    for c in ins[7:]:
+        c.wait()
     lax.fori_loop(0, FIRST, to_packets(pka, 0), 0)
     scatter(pka, sta, sa_send, sa_recv)
     lax.fori_loop(0, SECOND, to_packets(pkb, FIRST), 0)
@@ -383,7 +387,19 @@
         kept(j).start()
         return c
 
-    lax.fori_loop(0, CHUNKS, down, 0)
+    lax.fori_loop(0, CHUNKS - 1, down, 0)
+    end = CHUNKS - 1
+    d_load(end).wait()
+
+    def end_product(rows, i):
+        w = wbuf[pl.ds(B_BASE + 6 * B_ROWS, WIDTH), pl.ds(i * 256, 256)]
+        return jnp.dot(act[rows, :], w, preferred_element_type=F32).astype(BF)
+
+    for i in range(CHUNK // 256):
+        part[rows_of(other), pl.ds(end * CHUNK + i * 256, 256)] = end_product(rows_of(other), i)
+    halves(theirs, end, dn_send, dn_recv).start()
+    for i in range(CHUNK // 256):
+        mine[:, pl.ds(end * CHUNK + i * 256, 256)] = end_product(rows_of(core), i)
 
     for c in exchange:
         c.wait_send()
@@ -401,10 +417,15 @@
 
     def down_sent(j, c):
         halves(theirs, j, dn_send, dn_recv).wait()
+        return c
+
+    lax.fori_loop(0, CHUNKS, down_sent, 0)
+
+    def kept_all(j, c):
         kept(j).wait()
         return c
 
-    lax.fori_loop(0, CHUNKS, down_sent, 0)
+    lax.fori_loop(0, CHUNKS - 1, kept_all, 0)
 
 
 def last(mine, theirs, own_rows, kvo, og, lo, kc, vc, rows, og_row, kv_sem, og_sem, out_sem):

time: 59.6 us -> 58.5 us (0.982)
  Pallas kernels: 58.8 us -> 57.7 us
    pallas_call x1, Pallas kernels: 56.9 us -> 55.8 us  [per_device(): pl.pallas_call(kernel, out_shape=(vmem((ROWS, WIDTH), BF), vmem((ROWS, WI...]
where the time goes in v5:
time: 58.5 us; the launch traced here: 58.4 us
  Pallas kernels  57.7 us (99%)
  between operations  0.64 us (1%)
    pallas_call x1, Pallas kernels, per_device(): pl.pallas_call(kernel, out_shape=(vmem((ROWS, WIDTH), BF), vmem((ROWS, WI...  55.8 us
    pallas_call x1, Pallas kernels, per_device(): pl.pallas_call(last, out_shape=(jax.ShapeDtypeStruct((ROWS, WIDTH), BF),...  1.91 us

profile of v5, /device:TPU:1, one launch (start us, length us, event | category | flops | bytes accessed | tf_op | source)
XLA Modules:
  0.0 58.4 jit_solution(13199907116051417592)
XLA Ops:
  0.6 55.8 %layer.1 = (bf16[128,3584]{1,0:T(8,128)(2,1)S(1)}, bf16[128,3584]{1,0:T(8,128)(2,1)S(1)}, bf16[128,3584]{1,0:T(8,128)(2,1)S(1)}, bf16[8,128,256]{2,1,0:T(8,128)(2,1)S(1)}) custom-call(bf16[128,2048]{1,0:T(8,128)(2,1)} %q.1, bf16[128,1024]{1,0:T(8,128)(2,1)} %k.1, bf16[128,1024]{1,0:T(8,128)(2,1)} %v.1, bf16[128,3584]{1,0:T(8,128)(2,1)} %res.1, ...), custom_call_target="tpu_custom_call" | custom-call | tf_op jit(solution)/shard_map/layer/pallas_call | solution.py:481
  56.4 1.9 %last.1 = (bf16[128,3584]{1,0:T(8,128)(2,1)}, bf16[4,128,256]{2,1,0:T(8,128)(2,1)}, bf16[4,128,256]{2,1,0:T(8,128)(2,1)}) custom-call(bf16[128,3584]{1,0:T(8,128)(2,1)S(1)} %get-tuple-element.7.mine, bf16[128,3584]{1,0:T(8,128)(2,1)S(1)} %get-tuple-element.8.theirs, bf16[128,3584]{1,0:T(8,128)(2,1)S(1)} %get-tuple-element.9.own_rows, ...), custom_call_target="tpu_custom_call" | custom-call | tf_op jit(solution)/shard_map/last/pallas_call | solution.py:547

commit v6 on v5

--- a/solution.py
+++ b/solution.py
@@ -262,7 +262,16 @@
         halves(prec, j, pr_send, pr_recv).start()
         return c
 
-    lax.fori_loop(0, CHUNKS, project, 0)
+    lax.fori_loop(0, CHUNKS - 1, project, 0)
+    o_load(CHUNKS - 1).wait()
+
+    def end_project(rows):
+        w = wrows(B_BASE + (CHUNKS - 1) * HALF, HALF)[...]
+        part[rows, cols(CHUNKS - 1)] = jnp.dot(att[rows, :], w, preferred_element_type=F32).astype(BF)
+
+    end_project(rows_of(other))
+    halves(prec, CHUNKS - 1, pr_send, pr_recv).start()
+    end_project(rows_of(core))
     for unit in range(4):
         b_load((gw, uw)[unit % 2], unit // 2, unit).start()
 

time: 58.5 us -> 58.7 us (level)
  no operation moved by 1% of the time
where the time goes in v6:
time: 58.7 us; the launch traced here: 58.5 us
  Pallas kernels  57.9 us (99%)
  between operations  0.64 us (1%)
    pallas_call x1, Pallas kernels, per_device(): pl.pallas_call(kernel, out_shape=(vmem((ROWS, WIDTH), BF), vmem((ROWS, WI...  56 us
    pallas_call x1, Pallas kernels, per_device(): pl.pallas_call(last, out_shape=(jax.ShapeDtypeStruct((ROWS, WIDTH), BF),...  1.91 us

profile of v6, /device:TPU:1, one launch (start us, length us, event | category | flops | bytes accessed | tf_op | source)
XLA Modules:
  0.0 58.5 jit_solution(17618125513684556664)
XLA Ops:
  0.6 56.0 %layer.1 = (bf16[128,3584]{1,0:T(8,128)(2,1)S(1)}, bf16[128,3584]{1,0:T(8,128)(2,1)S(1)}, bf16[128,3584]{1,0:T(8,128)(2,1)S(1)}, bf16[8,128,256]{2,1,0:T(8,128)(2,1)S(1)}) custom-call(bf16[128,2048]{1,0:T(8,128)(2,1)} %q.1, bf16[128,1024]{1,0:T(8,128)(2,1)} %k.1, bf16[128,1024]{1,0:T(8,128)(2,1)} %v.1, bf16[128,3584]{1,0:T(8,128)(2,1)} %res.1, ...), custom_call_target="tpu_custom_call" | custom-call | tf_op jit(solution)/shard_map/layer/pallas_call | solution.py:490
  56.6 1.9 %last.1 = (bf16[128,3584]{1,0:T(8,128)(2,1)}, bf16[4,128,256]{2,1,0:T(8,128)(2,1)}, bf16[4,128,256]{2,1,0:T(8,128)(2,1)}) custom-call(bf16[128,3584]{1,0:T(8,128)(2,1)S(1)} %get-tuple-element.7.mine, bf16[128,3584]{1,0:T(8,128)(2,1)S(1)} %get-tuple-element.8.theirs, bf16[128,3584]{1,0:T(8,128)(2,1)S(1)} %get-tuple-element.9.own_rows, ...), custom_call_target="tpu_custom_call" | custom-call | tf_op jit(solution)/shard_map/last/pallas_call | solution.py:556
